TPU v7x, 32 devices: a whole 2x2x4 slice. The times are simulated.
32 devices in a mesh: lat: 8 (over y, x, core), lon: 4 (over z).
Axes of the slice: x: 2, y: 2, z: 4, core: 2. Of those that a mesh axis runs over, the one named last changes fastest.
Arguments:
- tracers: float32 [4, 4, 256, 720], P(None, None, 'lat', 'lon'), may hold values from -6 to 6
- courant: float32 [2, 4, 256, 720], P(None, None, 'lat', 'lon'), may hold values from -0.8 to 0.8
- cutoffs: int32 [256], replicated, may hold values from 1 to 360, as said below
Outputs:
- updated: float32 [4, 4, 256, 720], P(None, None, 'lat', 'lon')
- filtered_zonal: float32 [4, 256, 720], P(None, 'lat', 'lon')
Inputs may be any that keep to these rules, and one draw needn't show every extreme that they name: cutoffs[j] is 360 for every row j with min(j, 255 - j) >= 64, below 360 for all other rows, and 1 at the two pole rows.
All inputs are finite; a program needn't handle non-finite values.
Results may differ from a plain program's by a relative error of at most 0.0003.
Values sent between devices are 32-bit elements; how exact they have to be, the bound alone decides.
A program may use at most 64 MiB of HBM per device.

v0:
```python
import math

import jax
import jax.numpy as jnp
from jax import lax
from jax.sharding import PartitionSpec as P


def padded(cells, sides, width, closed):
    for axis, dim in sides:
        count = lax.axis_size(axis)
        ends = count if closed else count - 1
        head = lax.slice_in_dim(cells, 0, width, axis=dim)
        tail = lax.slice_in_dim(cells, cells.shape[dim] - width, cells.shape[dim], axis=dim)
        cells = jnp.concatenate(
            [
                lax.ppermute(tail, axis, [(i, (i + 1) % count) for i in range(ends)]),
                cells,
                lax.ppermute(head, axis, [((i + 1) % count, i) for i in range(ends)]),
            ],
            axis=dim,
        )
    return cells


def take_range(values, start, count, axis_index):
    return lax.slice_in_dim(values, start, start + count, axis=axis_index)


def ppm_flux(extended, courant_faces, axis_index):
    cell_count = extended.shape[axis_index] - 6
    edge_values = 7.0 / 12.0 * (
        take_range(extended, 1, cell_count + 3, axis_index)
        + take_range(extended, 2, cell_count + 3, axis_index)
    ) - 1.0 / 12.0 * (
        take_range(extended, 0, cell_count + 3, axis_index)
        + take_range(extended, 3, cell_count + 3, axis_index)
    )
    left_edge = take_range(edge_values, 0, cell_count + 2, axis_index)
    right_edge = take_range(edge_values, 1, cell_count + 2, axis_index)
    centre = take_range(extended, 2, cell_count + 2, axis_index)
    slopes = right_edge - left_edge
    curvature = 6.0 * centre - 3.0 * (left_edge + right_edge)
    upwind = take_range(right_edge, 0, cell_count + 1, axis_index) - 0.5 * courant_faces * (
        take_range(slopes, 0, cell_count + 1, axis_index)
        - (1.0 - courant_faces * (2.0 / 3.0)) * take_range(curvature, 0, cell_count + 1, axis_index)
    )
    downwind = take_range(left_edge, 1, cell_count + 1, axis_index) - 0.5 * courant_faces * (
        take_range(slopes, 1, cell_count + 1, axis_index)
        + (1.0 + courant_faces * (2.0 / 3.0)) * take_range(curvature, 1, cell_count + 1, axis_index)
    )
    return courant_faces * jnp.where(courant_faces > 0, upwind, downwind)


def metric_weights(first_row, row_count, grid_rows):
    faces = first_row + jnp.arange(-1, row_count, dtype=jnp.int32)
    centres = first_row + jnp.arange(row_count, dtype=jnp.int32)
    face_weight = jnp.sin(
        jnp.minimum(faces + 1, grid_rows - 1 - faces).astype(jnp.float32) * (math.pi / grid_rows)
    )
    cell_weight = jnp.sin(
        (jnp.minimum(centres, grid_rows - 1 - centres).astype(jnp.float32) + 0.5)
        * (math.pi / grid_rows)
    )
    return (face_weight, cell_weight)


def angle_table(first_ids, second_ids, period):
    product = first_ids[:, None] * second_ids[None, :] % period
    angles = product.astype(jnp.float32) * (2.0 * math.pi / period)
    return (jnp.cos(angles), jnp.sin(angles))


def spectral_lowpass(row_block, limits, outer_count):
    row_count, circle = row_block.shape
    inner_count = circle // outer_count
    highest = lax.Precision.HIGHEST
    grid_values = row_block.reshape(row_count, outer_count, inner_count)
    outer_ids = jnp.arange(outer_count, dtype=jnp.int32)
    inner_ids = jnp.arange(inner_count, dtype=jnp.int32)
    outer_cos, outer_sin = angle_table(outer_ids, outer_ids, outer_count)
    inner_cos, inner_sin = angle_table(inner_ids, inner_ids, inner_count)
    twiddle_cos, twiddle_sin = angle_table(inner_ids, outer_ids, circle)
    first_real = jnp.einsum("rab,ak->rbk", grid_values, outer_cos, precision=highest)
    first_imag = -jnp.einsum("rab,ak->rbk", grid_values, outer_sin, precision=highest)
    turned_real = first_real * twiddle_cos + first_imag * twiddle_sin
    turned_imag = first_imag * twiddle_cos - first_real * twiddle_sin
    coeff_real = jnp.einsum("rbk,bj->rjk", turned_real, inner_cos, precision=highest) + jnp.einsum(
        "rbk,bj->rjk", turned_imag, inner_sin, precision=highest
    )
    coeff_imag = jnp.einsum("rbk,bj->rjk", turned_imag, inner_cos, precision=highest) - jnp.einsum(
        "rbk,bj->rjk", turned_real, inner_sin, precision=highest
    )
    wavenumber = inner_ids[:, None] * outer_count + outer_ids[None, :]
    folded = jnp.minimum(wavenumber, circle - wavenumber)
    keep_mask = folded[None, :, :] <= limits[:, None, None]
    coeff_real = jnp.where(keep_mask, coeff_real, 0.0)
    coeff_imag = jnp.where(keep_mask, coeff_imag, 0.0)
    back_real = jnp.einsum("rjk,jb->rbk", coeff_real, inner_cos, precision=highest) - jnp.einsum(
        "rjk,jb->rbk", coeff_imag, inner_sin, precision=highest
    )
    back_imag = jnp.einsum("rjk,jb->rbk", coeff_imag, inner_cos, precision=highest) + jnp.einsum(
        "rjk,jb->rbk", coeff_real, inner_sin, precision=highest
    )
    reverted_real = back_real * twiddle_cos - back_imag * twiddle_sin
    reverted_imag = back_imag * twiddle_cos + back_real * twiddle_sin
    signal = jnp.einsum("rbk,ka->rab", reverted_real, outer_cos, precision=highest) - jnp.einsum(
        "rbk,ka->rab", reverted_imag, outer_sin, precision=highest
    )
    return (signal / circle).reshape(row_count, circle)


def circle_filter(row_block, limits, lon_groups):
    row_count = row_block.shape[0]
    whole_rows = lax.all_to_all(row_block, "lon", split_axis=0, concat_axis=1, tiled=True)
    held_count = row_count // lon_groups
    row_limits = lax.dynamic_slice_in_dim(limits, lax.axis_index("lon") * held_count, held_count)
    lowpass = spectral_lowpass(whole_rows, row_limits, lon_groups)
    lowpass = jnp.where((row_limits < whole_rows.shape[1] // 2)[:, None], lowpass, whole_rows)
    return lax.all_to_all(lowpass, "lon", split_axis=1, concat_axis=0, tiled=True)


def body(tracers, courant, cutoffs):
    levels, tracer_count, lat_rows, lon_cols = tracers.shape
    lon_groups = lax.axis_size("lon")
    lat_bands = lax.axis_size("lat")
    band_index = lax.axis_index("lat")
    grid_rows = lat_rows * lat_bands
    zonal = courant[0]
    meridional = courant[1]
    lat_stack = jnp.concatenate([tracers, meridional[:, None]], axis=1)
    lat_ext = padded(lat_stack, (("lat", 2),), 3, False)
    flat_count = levels * lat_rows
    flat_zonal = zonal.reshape(flat_count, lon_cols)
    local_limits = lax.dynamic_slice_in_dim(cutoffs, band_index * lat_rows, lat_rows)
    filtered_flat = circle_filter(flat_zonal, jnp.tile(local_limits, levels), lon_groups)
    filtered_zonal = filtered_flat.reshape(levels, lat_rows, lon_cols)
    lon_stack = jnp.concatenate([tracers, filtered_zonal[:, None]], axis=1)
    lon_ext = padded(lon_stack, (("lon", 3),), 3, True)
    flux_east = ppm_flux(
        lon_ext[:, :tracer_count], lon_ext[:, tracer_count:, :, 2 : lon_cols + 3], 3
    )
    face_weight, cell_weight = metric_weights(band_index * lat_rows, lat_rows, grid_rows)
    flux_north = (
        ppm_flux(lat_ext[:, :tracer_count], lat_ext[:, tracer_count:, 2 : lat_rows + 3, :], 2)
        * face_weight[None, None, :, None]
    )
    change = (
        flux_east[:, :, :, 1:]
        - flux_east[:, :, :, :-1]
        + (flux_north[:, :, 1:, :] - flux_north[:, :, :-1, :]) / cell_weight[None, None, :, None]
    )
    return (tracers - change, filtered_zonal)


def solution(mesh):
    in_specs = (P(None, None, "lat", "lon"), P(None, None, "lat", "lon"), P())
    out_specs = (P(None, None, "lat", "lon"), P(None, "lat", "lon"))
    return jax.shard_map(body, mesh=mesh, in_specs=in_specs, out_specs=out_specs, check_vma=False)
```

profile of v0, /device:TPU:0, one launch (start us, length us, event | category | flops | bytes accessed | tf_op | source)
XLA Modules:
  0.0 59.9 jit_solution(16525917794037167420)
XLA Ops:
  0.6 0.0 copy-start
  0.6 1.7 %slice_bitcast_fusion.1 = (f32[4,32,180]{2,1,0:T(8,128)}, f32[4,1,32,180]{3,2,1,0:T(8,128)S(1)}) fusion(f32[2,4,32,180]{3,2,1,0:T(8,128)} %param.4), kind=kLoop, calls=%fused_computation.113 | loop fusion | bytes 368640 | tf_op jit(solution)/shard_map/all_to_all | solution.py:115
  2.3 0.0 copy-done
  2.4 1.3 %collective-permute-start.3 = (f32[4,5,3,180]{3,2,1,0:T(4,128)S(1)}, f32[4,5,3,180]{3,2,1,0:T(4,128)S(1)}, u32[]{:S(2)}, u32[]{:S(2)}) collective-permute-start(f32[4,5,3,180]{3,2,1,0:T(4,128)S(1)} %get-tuple-element.15), channel_id=1, source_target_pairs={{4,0},{8,4},{12,8},{16,12},{20,16},{24,20},{28,24},{5,1},{9,5},{13... | collective-permute-start | bytes 129608 | tf_op jit(solution)/shard_map/ppermute | solution.py:19
  3.7 3.0 %collective-permute-start.2 = (f32[4,5,3,180]{3,2,1,0:T(4,128)S(1)}, f32[4,5,3,180]{3,2,1,0:T(4,128)S(1)}, u32[]{:S(2)}, u32[]{:S(2)}) collective-permute-start(f32[4,5,3,180]{3,2,1,0:T(4,128)S(1)} %get-tuple-element.14), channel_id=1, source_target_pairs={{0,4},{4,8},{8,12},{12,16},{16,20},{20,24},{24,28},{1,5},{5,9},{9,... | collective-permute-start | bytes 129608 | tf_op jit(solution)/shard_map/ppermute | solution.py:17
  6.7 6.4 %all-to-all-start = ((f32[4,32,180]{2,1,0:T(8,128)}), f32[4,32,180]{2,1,0:T(8,128)S(1)}, u32[]{:S(2)}, u32[]{:S(2)}) async-start(f32[4,32,180]{2,1,0:T(8,128)} %get-tuple-element.22), calls=%async_computation | async-start | bytes 262144 | tf_op jit(solution)/shard_map/all_to_all | solution.py:115
  13.1 0.1 fusion.114
  13.2 0.0 copy-start.1
  13.2 0.7 %copy-done.1 = s32[256]{0:T(256)S(1)} copy-done((s32[256]{0:T(256)S(1)}, s32[256]{0:T(256)}, u32[]{:S(2)}) %copy-start.1) | copy-done | bytes 1048
  13.9 0.1 dynamic_slice.6
  14.0 0.1 tile.10
  14.1 0.1 broadcast_compare_fusion
  14.2 0.0 collective-permute-done.3
  14.2 0.0 collective-permute-done.2
  14.2 0.1 pad_maximum_fusion
  14.3 0.3 fusion.20
  14.6 0.2 slice_subtract_fusion
  14.9 4.8 %all-to-all-done = f32[4,32,180]{2,1,0:T(8,128)S(1)} async-done(((f32[4,32,180]{2,1,0:T(8,128)}), f32[4,32,180]{2,1,0:T(8,128)S(1)}, u32[]{:S(2)}, u32[]{:S(2)}) %all-to-all-start) | async-done | bytes 92192 | tf_op jit(solution)/shard_map/all_to_all | solution.py:115
  19.7 0.4 convolution_bitcast_fusion
  20.1 0.4 multiply_add_fusion
  20.6 1.0 %fusion.47 = f32[180,32,4]{0,1,2:T(8,128)S(1)} fusion(f32[32,180,4]{1,2,0:T(4,128)S(1)} %get-tuple-element.21), kind=kOutput, calls=%fused_computation.82 | convolution fusion | flops 50058000 | bytes 184320 | tf_op jit(solution)/shard_map/rbk,bj->rjk/dot_general | solution.py:91
  21.6 1.0 %fusion.51 = f32[180,32,4]{0,1,2:T(8,128)S(1)} fusion(f32[32,180,4]{1,2,0:T(4,128)S(1)} %get-tuple-element.20), kind=kOutput, calls=%fused_computation.86 | convolution fusion | flops 50058000 | bytes 184320 | tf_op jit(solution)/shard_map/rbk,bj->rjk/dot_general | solution.py:88
  22.7 1.1 %fusion.5 = f32[32,180,4]{1,0,2:T(8,128)S(1)} fusion(f32[180,32,4]{0,1,2:T(8,128)S(1)} %fusion.47, f32[32,180,4]{1,2,0:T(4,128)S(1)} %get-tuple-element.20, s32[180,4]{0,1:T(4,128)S(1)} %subtract_minimum_fusion, s32[32]{0:T(128)S(1)} %get-tuple-element.7), kind=kOutput, calls=%fused_computation.11 | convolution fusion | flops 50127120 | bytes 279488 | tf_op jit(solution)/shard_map/rbk,bj->rjk/dot_general | solution.py:91
  23.8 1.1 %fusion.45 = f32[180,32,4]{0,1,2:T(8,128)S(1)} fusion(f32[32,180,4]{1,0,2:T(8,128)S(1)} %fusion.5), kind=kOutput, calls=%fused_computation.80 | convolution fusion | flops 50058000 | bytes 184320 | tf_op jit(solution)/shard_map/rjk,jb->rbk/dot_general | solution.py:102
  24.8 1.0 %fusion.7 = f32[32,180,4]{1,0,2:T(8,128)S(1)} fusion(f32[180,32,4]{0,1,2:T(8,128)S(1)} %fusion.51, f32[32,180,4]{1,2,0:T(4,128)S(1)} %get-tuple-element.21, s32[180,4]{0,1:T(4,128)S(1)} %subtract_minimum_fusion, s32[32]{0:T(128)S(1)} %get-tuple-element.7), kind=kOutput, calls=%fused_computation.14 | convolution fusion | flops 50127120 | bytes 279488 | tf_op jit(solution)/shard_map/rbk,bj->rjk/dot_general | solution.py:88
  25.9 1.0 %fusion.49 = f32[180,32,4]{0,1,2:T(8,128)S(1)} fusion(f32[32,180,4]{1,0,2:T(8,128)S(1)} %fusion.7), kind=kOutput, calls=%fused_computation.84 | convolution fusion | flops 50058000 | bytes 184320 | tf_op jit(solution)/shard_map/rjk,jb->rbk/dot_general | solution.py:99
  26.9 1.1 %convolution_add_fusion = f32[180,32,4]{0,1,2:T(8,128)S(1)} fusion(f32[180,32,4]{0,1,2:T(8,128)S(1)} %fusion.45, f32[32,180,4]{1,0,2:T(8,128)S(1)} %fusion.7), kind=kOutput, calls=%fused_computation.7 | convolution fusion | flops 50081040 | bytes 276480 | tf_op jit(solution)/shard_map/rjk,jb->rbk/dot_general | solution.py:102
  28.0 1.1 %add_bitcast_fusion.2 = (f32[32,180,4]{1,0,2:T(8,128)S(1)}, f32[32,180,4]{1,0,2:T(8,128)S(1)}) fusion(f32[180,32,4]{0,1,2:T(8,128)S(1)} %convolution_add_fusion, f32[180,4]{0,1:T(4,128)S(1)} %get-tuple-element.30, f32[180,4]{0,1:T(4,128)S(1)} %get-tuple-element.31, f32[180,32,4]{0,1,2:T(8,128)S(1)} %fusion.49, f32[32,180,4]{1,0,2:T(8,128)S(1)} %fusion.5), kind=kOutput, calls=%fused_computation.109 | convolution fusion | flops 50219280 | bytes 466560 | tf_op jit(solution)/shard_map/rjk,jb->rbk/dot_general | solution.py:99
  29.0 0.4 fusion.69
  29.5 0.5 fusion.3
  30.0 0.7 %copy.21 = f32[32,4,180]{2,0,1:T(8,128)} copy(f32[32,4,180]{2,1,0:T(4,128)S(1)} %fusion.3) | data formatting | bytes 184320 | tf_op jit(solution)/shard_map/jit(_where)/select_n | solution.py:119
  30.6 3.4 %all-to-all-start.1 = ((f32[32,4,180]{2,0,1:T(8,128)}), f32[32,4,180]{2,0,1:T(8,128)S(1)}, u32[]{:S(2)}, u32[]{:S(2)}) async-start(f32[32,4,180]{2,0,1:T(8,128)} %copy.21), calls=%async_computation.1 | async-start | bytes 262144 | tf_op jit(solution)/shard_map/all_to_all | solution.py:120
  34.1 6.2 %all-to-all-done.1 = f32[32,4,180]{2,0,1:T(8,128)S(1)} async-done(((f32[32,4,180]{2,0,1:T(8,128)}), f32[32,4,180]{2,0,1:T(8,128)S(1)}, u32[]{:S(2)}, u32[]{:S(2)}) %all-to-all-start.1) | async-done | bytes 92192 | tf_op jit(solution)/shard_map/all_to_all | solution.py:120
  40.3 0.2 fusion.38
  40.4 1.7 %collective-permute-start.1 = (f32[4,5,32,3]{3,2,1,0:T(8,128)S(1)}, f32[4,5,32,3]{3,2,1,0:T(8,128)S(1)}, u32[]{:S(2)}, u32[]{:S(2)}) collective-permute-start(f32[4,5,32,3]{3,2,1,0:T(8,128)S(1)} %get-tuple-element.11), channel_id=1, source_target_pairs={{1,0},{2,1},{3,2},{0,3},{5,4},{6,5},{7,6},{4,7},{9,8},{10,9},{11,1... | collective-permute-start | bytes 23048 | tf_op jit(solution)/shard_map/ppermute | solution.py:19
  42.1 0.4 collective-permute-start
  42.5 0.4 fusion.13
  42.9 7.3 %collective-permute-done.1 = f32[4,5,32,3]{3,2,1,0:T(8,128)S(1)} collective-permute-done((f32[4,5,32,3]{3,2,1,0:T(8,128)S(1)}, f32[4,5,32,3]{3,2,1,0:T(8,128)S(1)}, u32[]{:S(2)}, u32[]{:S(2)}) %collective-permute-start.1) | collective-permute-done | bytes 7712 | tf_op jit(solution)/shard_map/ppermute | solution.py:19
  50.2 6.2 %collective-permute-done = f32[4,5,32,3]{3,2,1,0:T(8,128)S(1)} collective-permute-done((f32[4,5,32,3]{3,2,1,0:T(8,128)S(1)}, f32[4,5,32,3]{3,2,1,0:T(8,128)S(1)}, u32[]{:S(2)}, u32[]{:S(2)}) %collective-permute-start) | collective-permute-done | bytes 7712 | tf_op jit(solution)/shard_map/ppermute | solution.py:17
  56.4 0.3 pad_maximum_fusion.5
  56.7 0.5 fusion.36
  57.3 0.3 slice_subtract_fusion.3
  57.6 0.1 compare_bitcast_fusion.1
  57.8 0.5 fusion.29
  58.3 1.0 %fusion.24 = f32[4,4,32,180]{3,2,1,0:T(8,128)} fusion(f32[4,4,32,180]{3,2,1,0:T(8,128)S(1)} %copy-done, f32[4,4,33,180]{3,2,1,0:T(8,128)S(1)} %fusion.13, f32[4,4,32,181]{3,2,1,0:T(8,128)S(1)} %fusion.29, f32[32]{0:T(128)S(1)} %fusion.125), kind=kLoop, calls=%fused_computation.47 | loop fusion | flops 460800 | bytes 2211968 | tf_op jit(solution)/shard_map/sub | solution.py:153
  59.3 0.7 %copy.47 = f32[4,32,180]{2,1,0:T(8,128)} copy(f32[4,32,180]{2,1,0:T(8,128)S(1)} %bitcast.95) | data formatting | bytes 184320
  (9 shorter events, 0.3 us)
Async XLA Ops:
  0.6 1.7 %copy-start = (f32[4,4,32,180]{3,2,1,0:T(8,128)S(1)}, f32[4,4,32,180]{3,2,1,0:T(8,128)}, u32[]{:S(2)}) copy-start(f32[4,4,32,180]{3,2,1,0:T(8,128)} %param.3) | copy-start | bytes 1105924
  2.4 11.8 %collective-permute-start.3 = (f32[4,5,3,180]{3,2,1,0:T(4,128)S(1)}, f32[4,5,3,180]{3,2,1,0:T(4,128)S(1)}, u32[]{:S(2)}, u32[]{:S(2)}) collective-permute-start(f32[4,5,3,180]{3,2,1,0:T(4,128)S(1)} %get-tuple-element.15), channel_id=1, source_target_pairs={{4,0},{8,4},{12,8},{16,12},{20,16},{24,20},{28,24},{5,1},{9,5},{13... | collective-permute-start | bytes 129608 | tf_op jit(solution)/shard_map/ppermute | solution.py:19
  3.7 10.5 %collective-permute-start.2 = (f32[4,5,3,180]{3,2,1,0:T(4,128)S(1)}, f32[4,5,3,180]{3,2,1,0:T(4,128)S(1)}, u32[]{:S(2)}, u32[]{:S(2)}) collective-permute-start(f32[4,5,3,180]{3,2,1,0:T(4,128)S(1)} %get-tuple-element.14), channel_id=1, source_target_pairs={{0,4},{4,8},{8,12},{12,16},{16,20},{20,24},{24,28},{1,5},{5,9},{9,... | collective-permute-start | bytes 129608 | tf_op jit(solution)/shard_map/ppermute | solution.py:17
  6.7 13.0 %all-to-all-start = ((f32[4,32,180]{2,1,0:T(8,128)}), f32[4,32,180]{2,1,0:T(8,128)S(1)}, u32[]{:S(2)}, u32[]{:S(2)}) async-start(f32[4,32,180]{2,1,0:T(8,128)} %get-tuple-element.22), calls=%async_computation | async-start | bytes 262144 | tf_op jit(solution)/shard_map/all_to_all | solution.py:115
  13.2 0.7 %copy-start.1 = (s32[256]{0:T(256)S(1)}, s32[256]{0:T(256)}, u32[]{:S(2)}) copy-start(s32[256]{0:T(256)} %param.5) | copy-start | bytes 3076
  30.6 9.6 %all-to-all-start.1 = ((f32[32,4,180]{2,0,1:T(8,128)}), f32[32,4,180]{2,0,1:T(8,128)S(1)}, u32[]{:S(2)}, u32[]{:S(2)}) async-start(f32[32,4,180]{2,0,1:T(8,128)} %copy.21), calls=%async_computation.1 | async-start | bytes 262144 | tf_op jit(solution)/shard_map/all_to_all | solution.py:120
  40.4 9.8 %collective-permute-start.1 = (f32[4,5,32,3]{3,2,1,0:T(8,128)S(1)}, f32[4,5,32,3]{3,2,1,0:T(8,128)S(1)}, u32[]{:S(2)}, u32[]{:S(2)}) collective-permute-start(f32[4,5,32,3]{3,2,1,0:T(8,128)S(1)} %get-tuple-element.11), channel_id=1, source_target_pairs={{1,0},{2,1},{3,2},{0,3},{5,4},{6,5},{7,6},{4,7},{9,8},{10,9},{11,1... | collective-permute-start | bytes 23048 | tf_op jit(solution)/shard_map/ppermute | solution.py:19
  42.1 14.3 %collective-permute-start = (f32[4,5,32,3]{3,2,1,0:T(8,128)S(1)}, f32[4,5,32,3]{3,2,1,0:T(8,128)S(1)}, u32[]{:S(2)}, u32[]{:S(2)}) collective-permute-start(f32[4,5,32,3]{3,2,1,0:T(8,128)S(1)} %get-tuple-element.10), channel_id=1, source_target_pairs={{0,1},{1,2},{2,3},{3,0},{4,5},{5,6},{6,7},{7,4},{8,9},{9,10},{10,1... | collective-permute-start | bytes 23048 | tf_op jit(solution)/shard_map/ppermute | solution.py:17
where the time goes:
time: 60.3 us; the launch traced here: 59.9 us
  waiting for transfers between devices  24.5 us (41%)
  starting transfers between devices  16.2 us (27%)
  matrix products  10.1 us (17%)
  other arithmetic  4.35 us (7%)
  local copies, waits for them, and re-layouts  3.88 us (6%)
  between operations  0.88 us (1%)
    ppermute x2, waiting for transfers between devices, padded(): lax.ppermute(head, axis, [((i + 1) % count, i) for i in range(ends)])  7.29 us
    all_to_all x1, starting transfers between devices, circle_filter(): lax.all_to_all(row_block, 'lon', split_axis=0, concat_axis=1, tiled=True)  6.36 us
    ppermute x2, waiting for transfers between devices, padded(): lax.ppermute(tail, axis, [(i, (i + 1) % count) for i in range(ends)])  6.19 us
    all_to_all x1, waiting for transfers between devices, circle_filter(): lax.all_to_all(lowpass, 'lon', split_axis=1, concat_axis=0, tiled=True)  6.16 us
    all_to_all x1, waiting for transfers between devices, circle_filter(): lax.all_to_all(row_block, 'lon', split_axis=0, concat_axis=1, tiled=True)  4.84 us
    ppermute x2, starting transfers between devices, padded(): lax.ppermute(tail, axis, [(i, (i + 1) % count) for i in range(ends)])  3.45 us
    all_to_all x1, starting transfers between devices, circle_filter(): lax.all_to_all(lowpass, 'lon', split_axis=1, concat_axis=0, tiled=True)  3.43 us
    ppermute x2, starting transfers between devices, padded(): lax.ppermute(head, axis, [((i + 1) % count, i) for i in range(ends)])  2.95 us
  transfers between devices with their start and end apart: 6, of which 4 were waited for; matrix products, arithmetic and copies ran while one was open for 2% of the time, Pallas kernels for 0%

commit v1 on v0

--- a/solution.py
+++ b/solution.py
@@ -1,6 +1,7 @@
 import math
 
 import jax
+import numpy as np
 import jax.numpy as jnp
 from jax import lax
 from jax.sharding import PartitionSpec as P
@@ -110,14 +111,65 @@
     return (signal / circle).reshape(row_count, circle)
 
 
+def dense_tables(circle):
+    half = circle // 2
+    cell_ids = np.arange(circle, dtype=np.int64)
+    cos_ids = np.arange(half + 1, dtype=np.int64)
+    sin_ids = np.arange(1, half, dtype=np.int64)
+    forward = np.concatenate(
+        [
+            np.cos(2.0 * np.pi * ((cell_ids[:, None] * cos_ids[None, :]) % circle) / circle),
+            np.sin(2.0 * np.pi * ((cell_ids[:, None] * sin_ids[None, :]) % circle) / circle),
+        ],
+        axis=1,
+    )
+    out_ids = np.arange(-1, circle, dtype=np.int64)
+    cos_scale = np.where((cos_ids == 0) | (cos_ids == half), 1.0, 2.0) / circle
+    inverse = np.concatenate(
+        [
+            cos_scale[:, None]
+            * np.cos(2.0 * np.pi * ((cos_ids[:, None] * out_ids[None, :]) % circle) / circle),
+            (2.0 / circle)
+            * np.sin(2.0 * np.pi * ((sin_ids[:, None] * out_ids[None, :]) % circle) / circle),
+        ],
+        axis=0,
+    )
+    wavenumber = np.concatenate([cos_ids, sin_ids]).astype(np.int32)
+    return (
+        jnp.asarray(forward.astype(np.float32)),
+        jnp.asarray(inverse.astype(np.float32)),
+        jnp.asarray(wavenumber),
+    )
+
+
+def dense_lowpass(row_block, limits):
+    circle = row_block.shape[1]
+    forward, inverse, wavenumber = dense_tables(circle)
+    highest = lax.Precision.HIGHEST
+    coeff = jnp.dot(row_block, forward, precision=highest)
+    coeff = jnp.where(wavenumber[None, :] <= limits[:, None], coeff, 0.0)
+    return jnp.dot(coeff, inverse, precision=highest)
+
+
 def circle_filter(row_block, limits, lon_groups):
-    row_count = row_block.shape[0]
+    row_count, block_cols = row_block.shape
     whole_rows = lax.all_to_all(row_block, "lon", split_axis=0, concat_axis=1, tiled=True)
+    circle = whole_rows.shape[1]
     held_count = row_count // lon_groups
     row_limits = lax.dynamic_slice_in_dim(limits, lax.axis_index("lon") * held_count, held_count)
-    lowpass = spectral_lowpass(whole_rows, row_limits, lon_groups)
-    lowpass = jnp.where((row_limits < whole_rows.shape[1] // 2)[:, None], lowpass, whole_rows)
-    return lax.all_to_all(lowpass, "lon", split_axis=1, concat_axis=0, tiled=True)
+    whole_ext = jnp.concatenate([whole_rows[:, -1:], whole_rows], axis=1)
+    if circle <= 2048:
+        lowpass_ext = dense_lowpass(whole_rows, row_limits)
+    else:
+        lowpass = spectral_lowpass(whole_rows, row_limits, lon_groups)
+        lowpass_ext = jnp.concatenate([lowpass[:, -1:], lowpass], axis=1)
+    lowpass_ext = jnp.where((row_limits < circle // 2)[:, None], lowpass_ext, whole_ext)
+    slabs = jnp.stack(
+        [lowpass_ext[:, k * block_cols : (k + 1) * block_cols + 1] for k in range(lon_groups)],
+        axis=0,
+    )
+    back = lax.all_to_all(slabs, "lon", split_axis=0, concat_axis=1, tiled=True)
+    return back.reshape(row_count, block_cols + 1)
 
 
 def body(tracers, courant, cutoffs):
@@ -130,16 +182,14 @@
     meridional = courant[1]
     lat_stack = jnp.concatenate([tracers, meridional[:, None]], axis=1)
     lat_ext = padded(lat_stack, (("lat", 2),), 3, False)
+    lon_ext = padded(tracers, (("lon", 3),), 3, True)
     flat_count = levels * lat_rows
     flat_zonal = zonal.reshape(flat_count, lon_cols)
     local_limits = lax.dynamic_slice_in_dim(cutoffs, band_index * lat_rows, lat_rows)
     filtered_flat = circle_filter(flat_zonal, jnp.tile(local_limits, levels), lon_groups)
-    filtered_zonal = filtered_flat.reshape(levels, lat_rows, lon_cols)
-    lon_stack = jnp.concatenate([tracers, filtered_zonal[:, None]], axis=1)
-    lon_ext = padded(lon_stack, (("lon", 3),), 3, True)
-    flux_east = ppm_flux(
-        lon_ext[:, :tracer_count], lon_ext[:, tracer_count:, :, 2 : lon_cols + 3], 3
-    )
+    zonal_faces = filtered_flat.reshape(levels, 1, lat_rows, lon_cols + 1)
+    filtered_zonal = zonal_faces[:, 0, :, 1:]
+    flux_east = ppm_flux(lon_ext, zonal_faces, 3)
     face_weight, cell_weight = metric_weights(band_index * lat_rows, lat_rows, grid_rows)
     flux_north = (
         ppm_flux(lat_ext[:, :tracer_count], lat_ext[:, tracer_count:, 2 : lat_rows + 3, :], 2)

time: 60.3 us -> 60.6 us (level)
  waiting for transfers between devices: 24.5 us -> 11.4 us
  other arithmetic: 4.35 us -> 14.5 us
  local copies, waits for them, and re-layouts: 3.88 us -> 10.3 us
  matrix products: 10.1 us -> 4.33 us
  starting transfers between devices: 16.2 us -> 18.5 us
    ppermute x2, waiting for transfers between devices: 7.29 us -> 0.62 us  [padded(): lax.ppermute(head, axis, [((i + 1) % count, i) for i in range(ends)])]
    dot_general x12 -> x2, matrix products: 10.1 us -> 4.33 us  [the longest x1 2.97 us: dense_lowpass(): coeff = jnp.dot(row_block, forward, precision=highest)]
    all_to_all x1, waiting for transfers between devices: 4.84 us -> 0.01 us  [circle_filter(): lax.all_to_all(row_block, 'lon', split_axis=0, concat_axis=1, tiled=True)]
    ppermute x2, starting transfers between devices: 2.95 us -> 6.42 us  [padded(): lax.ppermute(head, axis, [((i + 1) % count, i) for i in range(ends)])]
    all_to_all x1 -> x3, local copies, waits for them, and re-layouts: 1.7 us -> 5.04 us  [circle_filter(): lax.all_to_all(row_block, 'lon', split_axis=0, concat_axis=1, tiled=True)]
    mul x2, other arithmetic: 0.06 us -> 2.74 us  [ppm_flux(): 0.5 * courant_faces]
    slice x0 -> x2, local copies, waits for them, and re-layouts: none -> 2.1 us  [the longest x1 1.16 us: padded(): lax.slice_in_dim(cells, cells.shape[dim] - width, cells.shape[dim], axis=...]
    mul x1, other arithmetic: 0.39 us -> 2.4 us  [body(): ppm_flux(lat_ext[:, :tracer_count], lat_ext[:, tracer_count:, 2:lat_rows...]
  transfers between devices with their start and end apart: 6 -> 6, of which waited for: 4 -> 3; matrix products, arithmetic and copies ran while one was open for 2% -> 16% of each run, Pallas kernels for 0% -> 0%
where the time goes in v1:
time: 60.6 us; the launch traced here: 59.9 us
  starting transfers between devices  18.5 us (31%)
  other arithmetic  14.5 us (24%)
  waiting for transfers between devices  11.4 us (19%)
  local copies, waits for them, and re-layouts  10.3 us (17%)
  matrix products  4.33 us (7%)
  between operations  0.84 us (1%)
    ppermute x2, waiting for transfers between devices, padded(): lax.ppermute(tail, axis, [(i, (i + 1) % count) for i in range(ends)])  6.58 us
    ppermute x2, starting transfers between devices, padded(): lax.ppermute(head, axis, [((i + 1) % count, i) for i in range(ends)])  6.42 us
    all_to_all x1, starting transfers between devices, circle_filter(): lax.all_to_all(row_block, 'lon', split_axis=0, concat_axis=1, tiled=True)  5.09 us
    all_to_all x3, local copies, waits for them, and re-layouts, circle_filter(): lax.all_to_all(row_block, 'lon', split_axis=0, concat_axis=1, tiled=True)  5.04 us
    all_to_all x1, waiting for transfers between devices, circle_filter(): back = lax.all_to_all(slabs, 'lon', split_axis=0, concat_axis=1, tiled=True)  4.23 us
    all_to_all x1, starting transfers between devices, circle_filter(): back = lax.all_to_all(slabs, 'lon', split_axis=0, concat_axis=1, tiled=True)  3.95 us
    ppermute x2, starting transfers between devices, padded(): lax.ppermute(tail, axis, [(i, (i + 1) % count) for i in range(ends)])  3.04 us
    dot_general x1, matrix products, dense_lowpass(): coeff = jnp.dot(row_block, forward, precision=highest)  2.97 us
  transfers between devices with their start and end apart: 6, of which 3 were waited for; matrix products, arithmetic and copies ran while one was open for 16% of the time, Pallas kernels for 0%

profile of v1, /device:TPU:0, one launch (start us, length us, event | category | flops | bytes accessed | tf_op | source)
XLA Modules:
  0.0 59.9 jit_solution(7719575748991586604)
XLA Ops:
  0.6 0.0 copy-start
  0.6 0.0 copy-start.10
  0.7 1.7 %slice_bitcast_fusion.2 = (f32[4,32,180]{2,1,0:T(8,128)}, f32[4,1,32,180]{3,2,1,0:T(8,128)S(1)}) fusion(f32[2,4,32,180]{3,2,1,0:T(8,128)} %param.7), kind=kLoop, calls=%fused_computation.59 | loop fusion | bytes 368640 | tf_op jit(solution)/shard_map/all_to_all | solution.py:156
  2.4 1.1 %pad_maximum_fusion.9 = (f32[4,5,3,180]{3,2,1,0:T(4,128)S(1)}, f32[4,5,3,180]{3,2,1,0:T(4,128)S(1)}) fusion(f32[4,1,32,180]{3,2,1,0:T(8,128)S(1)} %get-tuple-element.15, f32[4,4,32,180]{3,2,1,0:T(8,128)} %param.6), kind=kLoop, calls=%fused_computation.63 | loop fusion | flops 21600 | bytes 547200 | tf_op jit(solution)/shard_map/slice | solution.py:15
  3.4 1.3 %collective-permute-start.3 = (f32[4,5,3,180]{3,2,1,0:T(4,128)S(1)}, f32[4,5,3,180]{3,2,1,0:T(4,128)S(1)}, u32[]{:S(2)}, u32[]{:S(2)}) collective-permute-start(f32[4,5,3,180]{3,2,1,0:T(4,128)S(1)} %get-tuple-element.9), channel_id=1, source_target_pairs={{4,0},{8,4},{12,8},{16,12},{20,16},{24,20},{28,24},{5,1},{9,5},{13... | collective-permute-start | bytes 129608 | tf_op jit(solution)/shard_map/ppermute | solution.py:20
  4.7 3.0 %collective-permute-start.2 = (f32[4,5,3,180]{3,2,1,0:T(4,128)S(1)}, f32[4,5,3,180]{3,2,1,0:T(4,128)S(1)}, u32[]{:S(2)}, u32[]{:S(2)}) collective-permute-start(f32[4,5,3,180]{3,2,1,0:T(4,128)S(1)} %get-tuple-element.8), channel_id=1, source_target_pairs={{0,4},{4,8},{8,12},{12,16},{16,20},{20,24},{24,28},{1,5},{5,9},{9,... | collective-permute-start | bytes 129608 | tf_op jit(solution)/shard_map/ppermute | solution.py:18
  7.8 1.2 %fusion.34 = (f32[4,4,32,3]{3,2,1,0:T(8,128)S(1)}, f32[4,4,32,3]{3,2,1,0:T(8,128)S(1)}) fusion(f32[4,4,32,180]{3,2,1,0:T(8,128)} %param.6), kind=kLoop, calls=%fused_computation.77 | loop fusion | bytes 24576 | tf_op jit(solution)/shard_map/slice | solution.py:15
  8.9 5.1 %collective-permute-start.1 = (f32[4,4,32,3]{3,2,1,0:T(8,128)S(1)}, f32[4,4,32,3]{3,2,1,0:T(8,128)S(1)}, u32[]{:S(2)}, u32[]{:S(2)}) collective-permute-start(f32[4,4,32,3]{3,2,1,0:T(8,128)S(1)} %get-tuple-element.13), channel_id=1, source_target_pairs={{1,0},{2,1},{3,2},{0,3},{5,4},{6,5},{7,6},{4,7},{9,8},{10,9},{11,1... | collective-permute-start | bytes 18440 | tf_op jit(solution)/shard_map/ppermute | solution.py:20
  14.1 0.0 collective-permute-start
  14.1 5.1 %all-to-all-start = ((f32[4,32,180]{2,1,0:T(8,128)}), f32[4,32,180]{2,1,0:T(8,128)}, u32[]{:S(2)}, u32[]{:S(2)}) async-start(f32[4,32,180]{2,1,0:T(8,128)} %get-tuple-element.14), calls=%async_computation | async-start | bytes 262144 | tf_op jit(solution)/shard_map/all_to_all | solution.py:156
  19.2 0.1 dynamic_slice.6
  19.3 0.1 tile.10
  19.4 0.1 broadcast_compare_fusion.1
  19.5 0.6 fusion.33
  20.0 0.6 %collective-permute-done.1 = f32[4,4,32,3]{3,2,1,0:T(8,128)S(1)} collective-permute-done((f32[4,4,32,3]{3,2,1,0:T(8,128)S(1)}, f32[4,4,32,3]{3,2,1,0:T(8,128)S(1)}, u32[]{:S(2)}, u32[]{:S(2)}) %collective-permute-start.1) | collective-permute-done | bytes 6176 | tf_op jit(solution)/shard_map/ppermute | solution.py:20
  20.7 6.6 %collective-permute-done = f32[4,4,32,3]{3,2,1,0:T(8,128)S(1)} collective-permute-done((f32[4,4,32,3]{3,2,1,0:T(8,128)S(1)}, f32[4,4,32,3]{3,2,1,0:T(8,128)S(1)}, u32[]{:S(2)}, u32[]{:S(2)}) %collective-permute-start) | collective-permute-done | bytes 6176 | tf_op jit(solution)/shard_map/ppermute | solution.py:18
  27.2 0.3 pad_maximum_fusion.5
  27.5 0.6 fusion.28
  28.1 1.1 %slice_subtract_fusion.3 = (f32[4,4,32,182]{3,2,1,0:T(8,128)S(1)}, f32[4,4,32,182]{3,2,1,0:T(8,128)}) fusion(f32[4,4,32,183]{3,2,1,0:T(8,128)S(1)} %fusion.28, f32[4,4,32,186]{3,2,1,0:T(8,128)S(1)} %pad_maximum_fusion.5), kind=kLoop, calls=%fused_computation.50 | loop fusion | flops 465920 | bytes 1863680 | tf_op jit(solution)/shard_map/sub | solution.py:43
  29.2 0.0 collective-permute-done.3
  29.2 0.0 collective-permute-done.2
  29.2 0.1 pad_maximum_fusion
  29.3 0.0 copy-done.2
  29.4 0.5 copy-done.6
  29.8 0.3 fusion.13
  30.1 0.0 copy-start.3
  30.1 0.0 copy-start.8
  30.2 0.2 slice_subtract_fusion
  30.4 0.7 %copy-done.3 = f32[4,1,32,180]{3,2,1,0:T(8,128)S(1)} copy-done((f32[4,1,32,180]{3,2,1,0:T(8,128)S(1)}, f32[4,1,32,180]{3,2,1,0:T(8,128)}, u32[]{:S(2)}) %copy-start.3) | copy-done | bytes 92184
  31.0 0.0 copy-done.7
  31.1 0.7 %compare_bitcast_fusion = (pred[4,33,180]{2,1,0:T(8,128)(4,1)}, f32[4,1,33,180]{3,2,1,0:T(8,128)}) fusion(f32[4,1,32,180]{3,2,1,0:T(8,128)S(1)} %copy-done.3, f32[4,4,32,180]{3,2,1,0:T(8,128)S(1)} %copy-done, f32[4,5,3,180]{3,2,1,0:T(4,128)S(1)} %copy-done.7), kind=kLoop, calls=%fused_computation.55 | loop fusion | flops 71280 | bytes 622800 | tf_op jit(solution)/shard_map/jit(_where)/broadcast_in_dim | solution.py:53
  31.8 1.7 %multiply_bitcast_fusion = (f32[4,33,180]{2,1,0:T(8,128)}, f32[4,33,180]{2,1,0:T(8,128)}, f32[4,33,180]{2,1,0:T(8,128)}) fusion(f32[4,1,33,180]{3,2,1,0:T(8,128)} %get-tuple-element.5), kind=kLoop, calls=%fused_computation.54 | loop fusion | flops 95040 | bytes 380160 | tf_op jit(solution)/shard_map/mul | solution.py:45
  33.5 0.0 all-to-all-done
  33.5 1.6 %copy.8 = f32[32,4,180]{2,1,0:T(4,128)} copy(f32[32,4,180]{2,0,1:T(8,128)} %bitcast.1) | data formatting | bytes 184320 | tf_op jit(solution)/shard_map/all_to_all | solution.py:156
  35.2 1.7 %all_to_all.26 = f32[32,720]{1,0:T(8,128)} reshape(f32[32,4,180]{2,1,0:T(4,128)} %copy.8) | data formatting | bytes 184320 | tf_op jit(solution)/shard_map/all_to_all | solution.py:156
  36.9 0.9 %slice.175 = f32[32,1]{1,0:T(8,128)S(1)} slice(f32[32,720]{1,0:T(8,128)} %all_to_all.26), slice={[0:32], [719:720]} | slice | bytes 256 | tf_op jit(solution)/shard_map/slice | solution.py:160
  37.8 3.0 %fusion = f32[32,720]{1,0:T(8,128)S(1)} fusion(f32[720,720]{1,0:T(8,128)} %constant.14.clone, f32[32,720]{1,0:T(8,128)} %all_to_all.26, s32[720]{0:T(1024)S(1)} %copy-done.8, s32[32]{0:T(128)S(1)} %get-tuple-element.3), kind=kOutput, calls=%fused_computation.2 | convolution fusion | flops 199111680 | bytes 2260928 | tf_op jit(solution)/shard_map/dot_general | solution.py:149
  40.8 1.4 %convolution_select_fusion = f32[32,721]{1,0:T(8,128)S(1)} fusion(f32[32,720]{1,0:T(8,128)S(1)} %fusion, f32[720,721]{1,0:T(8,128)S(1)} %copy-done.4, f32[32,720]{1,0:T(8,128)S(1)} %copy-done.5, f32[32,1]{1,0:T(8,128)S(1)} %slice.175, pred[32]{0:T(512)(128)(4,1)S(1)} %get-tuple-element.2), kind=kOutput, calls=%fused_computation | convolution fusion | flops 199388224 | bytes 2353248 | tf_op jit(solution)/shard_map/dot_general | solution.py:151
  42.2 0.1 slice_bitcast_fusion.6
  42.3 0.7 %pad_maximum_fusion.7 = f32[4,32,181]{2,1,0:T(8,128)} fusion(f32[1,32,181]{2,1,0:T(8,128)S(1)} %get-tuple-element.23, f32[1,32,181]{2,1,0:T(8,128)S(1)} %get-tuple-element.24, f32[1,32,181]{2,1,0:T(8,128)S(1)} %get-tuple-element.25, f32[1,32,181]{2,1,0:T(8,128)S(1)} %get-tuple-element.22), kind=kLoop, calls=%fused_computation.57 | loop fusion | flops 69504 | bytes 185344 | tf_op jit(solution)/shard_map/stack | solution.py:167
  42.9 4.0 %all-to-all-start.1 = ((f32[4,32,181]{2,1,0:T(8,128)}), f32[4,32,181]{2,1,0:T(8,128)}, u32[]{:S(2)}, u32[]{:S(2)}) async-start(f32[4,32,181]{2,1,0:T(8,128)} %pad_maximum_fusion.7), calls=%async_computation.1 | async-start | bytes 262144 | tf_op jit(solution)/shard_map/all_to_all | solution.py:171
  46.9 2.4 %fusion.6 = f32[4,4,33,180]{3,2,1,0:T(8,128)} fusion(f32[4,4,34,180]{3,2,1,0:T(8,128)S(1)} %get-tuple-element.7, f32[4,4,34,180]{3,2,1,0:T(8,128)S(1)} %get-tuple-element.6, f32[4,4,35,180]{3,2,1,0:T(8,128)S(1)} %fusion.13, f32[33]{0:T(128)S(1)} %multiply_sine_fusion, f32[4,33,180]{2,1,0:T(8,128)} %get-tuple-element.18, f32[4,33,180]{2,1,0:T(8,128)} %get-tuple-element.17, ...), kind=kLoop, calls=%fused_computation.10 | loop fusion | flops 1045440 | bytes 2685012 | tf_op jit(solution)/shard_map/mul | solution.py:195
  49.3 4.2 %all-to-all-done.1 = f32[4,32,181]{2,1,0:T(8,128)} async-done(((f32[4,32,181]{2,1,0:T(8,128)}), f32[4,32,181]{2,1,0:T(8,128)}, u32[]{:S(2)}, u32[]{:S(2)}) %all-to-all-start.1) | async-done | bytes 92704 | tf_op jit(solution)/shard_map/all_to_all | solution.py:171
  53.5 1.7 %slice_bitcast_fusion = f32[4,32,180]{2,1,0:T(8,128)} fusion(f32[4,1,32,181]{3,2,0,1:T(8,128)} %bitcast.13), kind=kLoop, calls=%fused_computation.56 | loop fusion | bytes 184320 | tf_op jit(solution)/shard_map/squeeze | solution.py:191
  55.2 1.0 %broadcast_multiply_fusion = (f32[4,32,181]{2,1,0:T(8,128)S(1)}, f32[4,32,181]{2,1,0:T(8,128)S(1)}, f32[4,32,181]{2,1,0:T(8,128)S(1)}) fusion(f32[4,32,181]{2,1,0:T(8,128)} %all-to-all-done.1), kind=kLoop, calls=%fused_computation.64 | loop fusion | flops 92672 | bytes 370688 | tf_op jit(solution)/shard_map/mul | solution.py:45
  56.2 0.9 %broadcast_compare_fusion = pred[4,32,181]{2,1,0:T(8,128)(4,1)S(1)} fusion(f32[4,32,181]{2,1,0:T(8,128)} %all-to-all-done.1), kind=kLoop, calls=%fused_computation.65 | loop fusion | flops 23168 | bytes 115840 | tf_op jit(solution)/shard_map/gt | solution.py:53
  57.1 1.8 %fusion.22 = f32[4,4,32,181]{3,2,1,0:T(8,128)S(1)} fusion(f32[4,4,32,182]{3,2,1,0:T(8,128)} %get-tuple-element.11, f32[4,4,32,182]{3,2,1,0:T(8,128)S(1)} %get-tuple-element.10, f32[4,4,32,183]{3,2,1,0:T(8,128)S(1)} %fusion.28, f32[4,32,181]{2,1,0:T(8,128)S(1)} %get-tuple-element.20, f32[4,32,181]{2,1,0:T(8,128)S(1)} %get-tuple-element.21, ...), kind=kLoop, calls=%fused_computation.37 | loop fusion | flops 926720 | bytes 2617984 | tf_op jit(solution)/shard_map/mul | solution.py:53
  58.9 1.0 %fusion.17 = f32[4,4,32,180]{3,2,1,0:T(8,128)} fusion(f32[4,4,32,180]{3,2,1,0:T(8,128)S(1)} %copy-done, f32[4,4,33,180]{3,2,1,0:T(8,128)S(1)} %copy-done.1, f32[4,4,32,181]{3,2,1,0:T(8,128)S(1)} %fusion.22, f32[32]{0:T(128)S(1)} %copy-done.9), kind=kLoop, calls=%fused_computation.30 | loop fusion | flops 460800 | bytes 2211968 | tf_op jit(solution)/shard_map/sub | solution.py:203
  (16 shorter events, 0.1 us)
Async XLA Ops:
  0.6 26.6 %copy-start = (f32[4,4,32,180]{3,2,1,0:T(8,128)S(1)}, f32[4,4,32,180]{3,2,1,0:T(8,128)}, u32[]{:S(2)}) copy-start(f32[4,4,32,180]{3,2,1,0:T(8,128)} %param.6) | copy-start | bytes 1105924
  0.6 18.6 %copy-start.10 = (s32[256]{0:T(256)S(1)}, s32[256]{0:T(256)}, u32[]{:S(2)}) copy-start(s32[256]{0:T(256)} %param.8) | copy-start | bytes 3076
  2.4 27.0 %copy-start.2 = (f32[4,1,32,180]{3,2,1,0:T(8,128)}, f32[4,1,32,180]{3,2,1,0:T(8,128)S(1)}, u32[]{:S(2)}) copy-start(f32[4,1,32,180]{3,2,1,0:T(8,128)S(1)} %get-tuple-element.15) | copy-start | bytes 276484
  3.4 25.8 %collective-permute-start.3 = (f32[4,5,3,180]{3,2,1,0:T(4,128)S(1)}, f32[4,5,3,180]{3,2,1,0:T(4,128)S(1)}, u32[]{:S(2)}, u32[]{:S(2)}) collective-permute-start(f32[4,5,3,180]{3,2,1,0:T(4,128)S(1)} %get-tuple-element.9), channel_id=1, source_target_pairs={{4,0},{8,4},{12,8},{16,12},{20,16},{24,20},{28,24},{5,1},{9,5},{13... | collective-permute-start | bytes 129608 | tf_op jit(solution)/shard_map/ppermute | solution.py:20
  4.7 24.5 %collective-permute-start.2 = (f32[4,5,3,180]{3,2,1,0:T(4,128)S(1)}, f32[4,5,3,180]{3,2,1,0:T(4,128)S(1)}, u32[]{:S(2)}, u32[]{:S(2)}) collective-permute-start(f32[4,5,3,180]{3,2,1,0:T(4,128)S(1)} %get-tuple-element.8), channel_id=1, source_target_pairs={{0,4},{4,8},{8,12},{12,16},{16,20},{20,24},{24,28},{1,5},{5,9},{9,... | collective-permute-start | bytes 129608 | tf_op jit(solution)/shard_map/ppermute | solution.py:18
  8.9 11.7 %collective-permute-start.1 = (f32[4,4,32,3]{3,2,1,0:T(8,128)S(1)}, f32[4,4,32,3]{3,2,1,0:T(8,128)S(1)}, u32[]{:S(2)}, u32[]{:S(2)}) collective-permute-start(f32[4,4,32,3]{3,2,1,0:T(8,128)S(1)} %get-tuple-element.13), channel_id=1, source_target_pairs={{1,0},{2,1},{3,2},{0,3},{5,4},{6,5},{7,6},{4,7},{9,8},{10,9},{11,1... | collective-permute-start | bytes 18440 | tf_op jit(solution)/shard_map/ppermute | solution.py:20
  14.1 13.2 %collective-permute-start = (f32[4,4,32,3]{3,2,1,0:T(8,128)S(1)}, f32[4,4,32,3]{3,2,1,0:T(8,128)S(1)}, u32[]{:S(2)}, u32[]{:S(2)}) collective-permute-start(f32[4,4,32,3]{3,2,1,0:T(8,128)S(1)} %get-tuple-element.12), channel_id=1, source_target_pairs={{0,1},{1,2},{2,3},{3,0},{4,5},{5,6},{6,7},{7,4},{8,9},{9,10},{10,1... | collective-permute-start | bytes 18440 | tf_op jit(solution)/shard_map/ppermute | solution.py:18
  14.1 19.5 %all-to-all-start = ((f32[4,32,180]{2,1,0:T(8,128)}), f32[4,32,180]{2,1,0:T(8,128)}, u32[]{:S(2)}, u32[]{:S(2)}) async-start(f32[4,32,180]{2,1,0:T(8,128)} %get-tuple-element.14), calls=%async_computation | async-start | bytes 262144 | tf_op jit(solution)/shard_map/all_to_all | solution.py:156
  29.2 0.6 %copy-start.6 = (f32[4,5,3,180]{3,2,1,0:T(4,128)}, f32[4,5,3,180]{3,2,1,0:T(4,128)S(1)}, u32[]{:S(2)}) copy-start(f32[4,5,3,180]{3,2,1,0:T(4,128)S(1)} %collective-permute-done.2) | copy-start | bytes 129604
  30.1 0.9 %copy-start.3 = (f32[4,1,32,180]{3,2,1,0:T(8,128)S(1)}, f32[4,1,32,180]{3,2,1,0:T(8,128)}, u32[]{:S(2)}) copy-start(f32[4,1,32,180]{3,2,1,0:T(8,128)} %copy-done.2) | copy-start | bytes 276484
  30.1 0.9 %copy-start.7 = (f32[4,5,3,180]{3,2,1,0:T(4,128)S(1)}, f32[4,5,3,180]{3,2,1,0:T(4,128)}, u32[]{:S(2)}) copy-start(f32[4,5,3,180]{3,2,1,0:T(4,128)} %copy-done.6) | copy-start | bytes 129604
  30.1 7.7 %copy-start.8 = (s32[720]{0:T(1024)S(1)}, s32[720]{0:T(1024)}, u32[]{:S(2)}) copy-start(s32[720]{0:T(1024)} %constant.16.clone) | copy-start | bytes 8644
  36.9 3.9 %copy-start.4 = (f32[720,721]{1,0:T(8,128)S(1)}, f32[720,721]{1,0:T(8,128)}, u32[]{:S(2)}) copy-start(f32[720,721]{1,0:T(8,128)} %constant.15.clone) | copy-start | bytes 6229444
  36.9 3.9 %copy-start.5 = (f32[32,720]{1,0:T(8,128)S(1)}, f32[32,720]{1,0:T(8,128)}, u32[]{:S(2)}) copy-start(f32[32,720]{1,0:T(8,128)} %all_to_all.26) | copy-start | bytes 276484
  42.9 10.6 %all-to-all-start.1 = ((f32[4,32,181]{2,1,0:T(8,128)}), f32[4,32,181]{2,1,0:T(8,128)}, u32[]{:S(2)}, u32[]{:S(2)}) async-start(f32[4,32,181]{2,1,0:T(8,128)} %pad_maximum_fusion.7), calls=%async_computation.1 | async-start | bytes 262144 | tf_op jit(solution)/shard_map/all_to_all | solution.py:171
  55.2 3.7 %copy-start.1 = (f32[4,4,33,180]{3,2,1,0:T(8,128)S(1)}, f32[4,4,33,180]{3,2,1,0:T(8,128)}, u32[]{:S(2)}) copy-start(f32[4,4,33,180]{3,2,1,0:T(8,128)} %fusion.6) | copy-start | bytes 1140484
  55.2 3.7 %copy-start.9 = (f32[32]{0:T(128)S(1)}, f32[32]{0:T(128)}, u32[]{:S(2)}) copy-start(f32[32]{0:T(128)} %fusion.33) | copy-start | bytes 388

commit v2 on v0

--- a/solution.py
+++ b/solution.py
@@ -1,6 +1,7 @@
 import math
 
 import jax
+import numpy as np
 import jax.numpy as jnp
 from jax import lax
 from jax.sharding import PartitionSpec as P
@@ -110,19 +111,31 @@
     return (signal / circle).reshape(row_count, circle)
 
 
-def circle_filter(row_block, limits, lon_groups):
-    row_count = row_block.shape[0]
-    whole_rows = lax.all_to_all(row_block, "lon", split_axis=0, concat_axis=1, tiled=True)
-    held_count = row_count // lon_groups
-    row_limits = lax.dynamic_slice_in_dim(limits, lax.axis_index("lon") * held_count, held_count)
-    lowpass = spectral_lowpass(whole_rows, row_limits, lon_groups)
-    lowpass = jnp.where((row_limits < whole_rows.shape[1] // 2)[:, None], lowpass, whole_rows)
-    return lax.all_to_all(lowpass, "lon", split_axis=1, concat_axis=0, tiled=True)
+def dense_tables(circle):
+    half = circle // 2
+    cell_ids = np.arange(-1, circle, dtype=np.int64)
+    cos_ids = np.arange(half + 1, dtype=np.int64)
+    sin_ids = np.arange(1, half, dtype=np.int64)
+    table = np.concatenate(
+        [
+            np.cos(2.0 * np.pi * ((cell_ids[:, None] * cos_ids[None, :]) % circle) / circle),
+            np.sin(2.0 * np.pi * ((cell_ids[:, None] * sin_ids[None, :]) % circle) / circle),
+        ],
+        axis=1,
+    )
+    wavenumber = np.concatenate([cos_ids, sin_ids])
+    scale = np.where((wavenumber == 0) | (wavenumber == half), 1.0, 2.0) / circle
+    return (
+        jnp.asarray(table.astype(np.float32)),
+        jnp.asarray(scale.astype(np.float32)),
+        jnp.asarray(wavenumber.astype(np.int32)),
+    )
 
 
 def body(tracers, courant, cutoffs):
     levels, tracer_count, lat_rows, lon_cols = tracers.shape
     lon_groups = lax.axis_size("lon")
+    lon_index = lax.axis_index("lon")
     lat_bands = lax.axis_size("lat")
     band_index = lax.axis_index("lat")
     grid_rows = lat_rows * lat_bands
@@ -132,14 +145,40 @@
     lat_ext = padded(lat_stack, (("lat", 2),), 3, False)
     flat_count = levels * lat_rows
     flat_zonal = zonal.reshape(flat_count, lon_cols)
+    edges = jnp.concatenate([tracers[..., :3], tracers[..., lon_cols - 3 :]], axis=-1)
+    gathered = lax.all_gather(flat_zonal, "lon", axis=0)
+    gathered_edges = lax.all_gather(edges, "lon", axis=0)
+    west_index = (lon_index + lon_groups - 1) % lon_groups
+    east_index = (lon_index + 1) % lon_groups
+    west = lax.dynamic_index_in_dim(gathered_edges, west_index, 0, keepdims=False)[..., 3:]
+    east = lax.dynamic_index_in_dim(gathered_edges, east_index, 0, keepdims=False)[..., :3]
+    lon_ext = jnp.concatenate([west, tracers, east], axis=-1)
     local_limits = lax.dynamic_slice_in_dim(cutoffs, band_index * lat_rows, lat_rows)
-    filtered_flat = circle_filter(flat_zonal, jnp.tile(local_limits, levels), lon_groups)
-    filtered_zonal = filtered_flat.reshape(levels, lat_rows, lon_cols)
-    lon_stack = jnp.concatenate([tracers, filtered_zonal[:, None]], axis=1)
-    lon_ext = padded(lon_stack, (("lon", 3),), 3, True)
-    flux_east = ppm_flux(
-        lon_ext[:, :tracer_count], lon_ext[:, tracer_count:, :, 2 : lon_cols + 3], 3
-    )
+    limits = jnp.tile(local_limits, levels)
+    circle = lon_cols * lon_groups
+    west_raw = lax.dynamic_index_in_dim(gathered, west_index, 0, keepdims=False)[:, -1:]
+    raw_ext = jnp.concatenate([west_raw, flat_zonal], axis=1)
+    if circle <= 2048:
+        table, scale, wavenumber = dense_tables(circle)
+        high = lax.Precision.HIGH
+        coeff = jnp.einsum(
+            "prm,pmw->rw",
+            gathered,
+            table[1:].reshape(lon_groups, lon_cols, circle),
+            precision=high,
+        )
+        coeff = jnp.where(wavenumber[None, :] <= limits[:, None], coeff * scale[None, :], 0.0)
+        local_table = lax.dynamic_slice_in_dim(table, lon_index * lon_cols, lon_cols + 1, axis=0)
+        lowpass_ext = jnp.einsum("rw,nw->rn", coeff, local_table, precision=high)
+    else:
+        whole_rows = jnp.transpose(gathered, (1, 0, 2)).reshape(flat_count, circle)
+        lowpass = spectral_lowpass(whole_rows, limits, lon_groups)
+        lowpass = jnp.concatenate([lowpass[:, -1:], lowpass], axis=1)
+        lowpass_ext = lax.dynamic_slice_in_dim(lowpass, lon_index * lon_cols, lon_cols + 1, axis=1)
+    filtered_flat = jnp.where((limits < circle // 2)[:, None], lowpass_ext, raw_ext)
+    zonal_faces = filtered_flat.reshape(levels, 1, lat_rows, lon_cols + 1)
+    filtered_zonal = zonal_faces[:, 0, :, 1:]
+    flux_east = ppm_flux(lon_ext, zonal_faces, 3)
     face_weight, cell_weight = metric_weights(band_index * lat_rows, lat_rows, grid_rows)
     flux_north = (
         ppm_flux(lat_ext[:, :tracer_count], lat_ext[:, tracer_count:, 2 : lat_rows + 3, :], 2)

time: 60.3 us -> 52.8 us (0.88)
  blocking collectives: 0 us -> 30.6 us
  waiting for transfers between devices: 24.5 us -> 0.01 us
  starting transfers between devices: 16.2 us -> 4.32 us
  matrix products: 10.1 us -> 3.63 us
  other arithmetic: 4.35 us -> 7.38 us
  local copies, waits for them, and re-layouts: 3.88 us -> 5.68 us
    all_gather x0 -> x2, blocking collectives: none -> 30.6 us  [the longest x1 17 us: body(): gathered = lax.all_gather(flat_zonal, 'lon', axis=0)]
    all_to_all x2 -> x0, waiting for transfers between devices: 11 us -> none  [the longest x1 6.16 us: circle_filter(): lax.all_to_all(lowpass, 'lon', split_axis=1, concat_axis=0, tiled=True)]
    all_to_all x2 -> x0, starting transfers between devices: 9.79 us -> none  [the longest x1 6.36 us: circle_filter(): lax.all_to_all(row_block, 'lon', split_axis=0, concat_axis=1, tiled=True)]
    ppermute x2 -> x1, waiting for transfers between devices: 7.29 us -> 0.01 us  [padded(): lax.ppermute(head, axis, [((i + 1) % count, i) for i in range(ends)])]
    dot_general x12 -> x2, matrix products: 10.1 us -> 3.63 us  [the longest x1 2.1 us: body(): jnp.einsum('prm,pmw->rw', gathered, table[1:].reshape(lon_groups, lon_col...]
    ppermute x2 -> x1, waiting for transfers between devices: 6.19 us -> 0.01 us  [padded(): lax.ppermute(tail, axis, [(i, (i + 1) % count) for i in range(ends)])]
    slice x0 -> x4, local copies, waits for them, and re-layouts: none -> 2.43 us  [the longest x1 1.16 us: body(): tracers[..., :3]]
    all_to_all x1 -> x0, local copies, waits for them, and re-layouts: 1.7 us -> none  [circle_filter(): lax.all_to_all(row_block, 'lon', split_axis=0, concat_axis=1, tiled=True)]
  transfers between devices with their start and end apart: 6 -> 2, of which waited for: 4 -> 0; matrix products, arithmetic and copies ran while one was open for 2% -> 19% of each run, Pallas kernels for 0% -> 0%
where the time goes in v2:
time: 52.8 us; the launch traced here: 52.5 us
  blocking collectives  30.6 us (58%)
  other arithmetic  7.38 us (14%)
  local copies, waits for them, and re-layouts  5.68 us (11%)
  starting transfers between devices  4.32 us (8%)
  matrix products  3.63 us (7%)
  between operations  0.94 us (2%)
    all_gather x1, blocking collectives, body(): gathered = lax.all_gather(flat_zonal, 'lon', axis=0)  17 us
    all_gather x1, blocking collectives, body(): gathered_edges = lax.all_gather(edges, 'lon', axis=0)  13.6 us
    ppermute x1, starting transfers between devices, padded(): lax.ppermute(tail, axis, [(i, (i + 1) % count) for i in range(ends)])  3.04 us
    dot_general x1, matrix products, body(): jnp.einsum('prm,pmw->rw', gathered, table[1:].reshape(lon_groups, lon_col...  2.1 us
    slice x1, other arithmetic, padded(): lax.slice_in_dim(cells, cells.shape[dim] - width, cells.shape[dim], axis=...  1.67 us
    sub x2, other arithmetic, ppm_flux(): 7.0 / 12.0  1.67 us
    dot_general x1, matrix products, body(): lowpass_ext = jnp.einsum('rw,nw->rn', coeff, local_table, precision=high)  1.53 us
    ppermute x1, starting transfers between devices, padded(): lax.ppermute(head, axis, [((i + 1) % count, i) for i in range(ends)])  1.28 us
  transfers between devices with their start and end apart: 2, of which 0 were waited for; matrix products, arithmetic and copies ran while one was open for 19% of the time, Pallas kernels for 0%

profile of v2, /device:TPU:0, one launch (start us, length us, event | category | flops | bytes accessed | tf_op | source)
XLA Modules:
  0.0 52.5 jit_solution(7654934705011135713)
XLA Ops:
  0.6 0.0 copy-start.1
  0.6 0.0 copy-start.3
  0.7 0.0 copy-start.4
  0.7 0.0 copy-start.5
  0.7 1.1 %fusion.39 = (f32[1,4,32,180]{3,2,1,0:T(8,128)S(1)}, f32[4,1,32,180]{3,2,1,0:T(8,128)S(1)}) fusion(f32[2,4,32,180]{3,2,1,0:T(8,128)} %param.7), kind=kLoop, calls=%fused_computation.80 | loop fusion | bytes 368640 | tf_op jit(solution)/shard_map/slice | solution.py:142
  1.8 1.7 %pad_maximum_fusion.8 = (f32[4,5,3,180]{3,2,1,0:T(4,128)}, f32[4,5,3,180]{3,2,1,0:T(4,128)}) fusion(f32[4,1,32,180]{3,2,1,0:T(8,128)S(1)} %get-tuple-element.13, f32[4,4,32,180]{3,2,1,0:T(8,128)} %param.6), kind=kLoop, calls=%fused_computation.65 | loop fusion | flops 21600 | bytes 547200 | tf_op jit(solution)/shard_map/slice | solution.py:15
  3.5 1.3 %collective-permute-start.1 = (f32[4,5,3,180]{3,2,1,0:T(4,128)}, f32[4,5,3,180]{3,2,1,0:T(4,128)}, u32[]{:S(2)}, u32[]{:S(2)}) collective-permute-start(f32[4,5,3,180]{3,2,1,0:T(4,128)} %get-tuple-element.7), channel_id=1, source_target_pairs={{4,0},{8,4},{12,8},{16,12},{20,16},{24,20},{28,24},{5,1},{9,5},{13... | collective-permute-start | bytes 129608 | tf_op jit(solution)/shard_map/ppermute | solution.py:20
  4.8 3.0 %collective-permute-start = (f32[4,5,3,180]{3,2,1,0:T(4,128)}, f32[4,5,3,180]{3,2,1,0:T(4,128)S(1)}, u32[]{:S(2)}, u32[]{:S(2)}) collective-permute-start(f32[4,5,3,180]{3,2,1,0:T(4,128)} %get-tuple-element.6), channel_id=1, source_target_pairs={{0,4},{4,8},{8,12},{12,16},{16,20},{20,24},{24,28},{1,5},{5,9},{9,... | collective-permute-start | bytes 129608 | tf_op jit(solution)/shard_map/ppermute | solution.py:18
  7.8 1.2 %fusion.38 = (f32[4,4,32,3]{3,2,1,0:T(8,128)S(1)}, f32[4,4,32,3]{3,2,1,0:T(8,128)S(1)}) fusion(f32[4,4,32,180]{3,2,1,0:T(8,128)} %param.6), kind=kLoop, calls=%fused_computation.79 | loop fusion | bytes 24576 | tf_op jit(solution)/shard_map/slice | solution.py:148
  9.1 0.7 %copy.29 = f32[1,128,180]{1,2,0:T(8,128)} copy(f32[1,128,180]{2,1,0:T(8,128)S(1)} %bitcast.45) | data formatting | bytes 184320 | tf_op jit(solution)/shard_map/all_gather;reshape;squeeze | solution.py:149
  9.8 17.0 %all_gather.9 = f32[4,128,180]{1,2,0:T(8,128)S(1)} all-gather(f32[1,128,180]{1,2,0:T(8,128)} %copy.29), channel_id=1, replica_groups=mesh['lat'=8,'lon'=4] {'lon'}, dimensions={0}, use_global_device_ids=true | all-gather | bytes 460800 | tf_op jit(solution)/shard_map/all_gather | solution.py:149
  26.8 0.0 copy-done.5
  26.8 0.1 dynamic_slice.17
  26.9 0.1 tile.10
  27.0 0.7 %copy.30 = f32[128,180]{0,1:T(8,128)} copy(f32[128,180]{1,0:T(8,128)S(1)} %bitcast.46) | data formatting | bytes 184320 | tf_op jit(solution)/shard_map/reshape;squeeze | solution.py:147
  27.7 0.0 copy-start.2
  27.8 0.0 copy-done.1
  27.8 0.0 copy-done.3
  27.8 0.0 copy-done.4
  27.8 2.1 %fusion.2 = f32[128,720]{0,1:T(8,128)S(1)} fusion(f32[4,180,720]{2,1,0:T(8,128)S(1)} %copy-done.1, f32[4,128,180]{1,2,0:T(8,128)S(1)} %all_gather.9, f32[720]{0:T(1024)S(1)} %copy-done.3, s32[128]{0:T(128)S(1)} %tile.10, s32[720]{0:T(1024)S(1)} %copy-done.4), kind=kOutput, calls=%fused_computation.3 | convolution fusion | flops 398407680 | bytes 2817152 | tf_op jit(solution)/shard_map/prm,pmw->rw/dot_general | solution.py:164
  29.9 0.0 copy-done.2
  29.9 0.0 copy-start
  29.9 1.5 %convolution_select_fusion = f32[128,181]{0,1:T(8,128)S(1)} fusion(f32[128,720]{0,1:T(8,128)S(1)} %fusion.2, f32[721,720]{1,0:T(8,128)} %constant.92.clone, s32[]{:T(128)S(6)} %select_n.44, f32[128,180]{0,1:T(8,128)S(1)} %copy-done.2, f32[128,1]{0,1:T(1,128)S(1)} %slice.171, pred[128]{0:T(512)(128)(4,1)S(1)} %broadcast_compare_fusion.1), kind=kOutput, calls=%fused_computation.4 | convolution fusion | flops 100132096 | bytes 1119364 | tf_op jit(solution)/shard_map/rw,nw->rn/dot_general | solution.py:172
  31.4 0.1 copy.31
  31.6 0.2 copy.39
  31.8 0.2 copy.38
  32.0 13.6 %all-gather = f32[16,4,32,6]{2,1,3,0:T(4,128)S(1)} all-gather(f32[4,4,32,6]{2,1,3,0:T(4,128)S(1)} %copy.34), channel_id=2, replica_groups=mesh['lat'=8,'lon'=4] {'lon'}, dimensions={0}, use_global_device_ids=true | all-gather | bytes 61440 | tf_op jit(solution)/shard_map/all_gather | solution.py:150
  45.6 0.2 copy.36
  45.8 0.2 copy.35
  45.9 0.1 slice.172
  46.1 0.0 copy-done
  46.1 0.3 pad_maximum_fusion.5
  46.4 0.6 %fusion.31 = f32[4,4,32,183]{3,2,1,0:T(8,128)S(1)} fusion(f32[4,4,32,186]{3,2,1,0:T(8,128)S(1)} %pad_maximum_fusion.5, f32[4,4,32,180]{3,2,1,0:T(8,128)S(1)} %copy-done, f32[4,4,32,3]{3,2,1,0:T(8,128)S(1)} %slice.172, f32[4,4,32,3]{3,2,1,0:T(8,128)S(1)} %bitcast.43), kind=kLoop, calls=%fused_computation.49 | loop fusion | flops 655872 | bytes 1505280 | tf_op jit(solution)/shard_map/sub | solution.py:33
  46.9 0.3 slice_subtract_fusion.3
  47.3 0.8 %slice_bitcast_fusion = f32[4,32,180]{2,1,0:T(8,128)} fusion(f32[4,1,32,181]{3,2,0,1:T(8,128)S(1)} %bitcast.40), kind=kLoop, calls=%fused_computation.59 | loop fusion | bytes 184320 | tf_op jit(solution)/shard_map/squeeze | solution.py:180
  48.0 0.5 fusion.25
  48.6 0.0 collective-permute-done.1
  48.6 0.0 collective-permute-done
  48.6 1.0 %pad_maximum_fusion = f32[4,5,38,180]{3,2,1,0:T(8,128)S(1)} fusion(f32[4,5,3,180]{3,2,1,0:T(4,128)} %collective-permute-done.1, f32[4,1,32,180]{3,2,1,0:T(8,128)S(1)} %get-tuple-element.13, f32[4,4,32,180]{3,2,1,0:T(8,128)S(1)} %copy-done, f32[4,5,3,180]{3,2,1,0:T(4,128)S(1)} %collective-permute-done), kind=kLoop, calls=%fused_computation.5 | loop fusion | flops 410400 | bytes 1094400 | tf_op jit(solution)/shard_map/concatenate | solution.py:16
  49.6 1.1 %fusion.15 = f32[4,4,35,180]{3,2,1,0:T(8,128)S(1)} fusion(f32[4,5,3,180]{3,2,1,0:T(4,128)} %collective-permute-done.1, f32[4,1,32,180]{3,2,1,0:T(8,128)S(1)} %get-tuple-element.13, f32[4,4,32,180]{3,2,1,0:T(8,128)S(1)} %copy-done, f32[4,5,3,180]{3,2,1,0:T(4,128)S(1)} %collective-permute-done, f32[4,5,38,180]{3,2,1,0:T(8,128)S(1)} %pad_maximum_fusion), kind=kLoop, calls=%fused_computation.22 | loop fusion | flops 907200 | bytes 1756800 | tf_op jit(solution)/shard_map/sub | solution.py:33
  50.7 0.2 slice_subtract_fusion
  51.0 0.4 fusion.8
  51.5 1.0 %fusion.20 = f32[4,4,32,180]{3,2,1,0:T(8,128)} fusion(f32[4,4,32,180]{3,2,1,0:T(8,128)S(1)} %copy-done, f32[4,4,33,180]{3,2,1,0:T(8,128)S(1)} %fusion.8, f32[4,4,32,181]{3,2,1,0:T(8,128)S(1)} %fusion.25, f32[32]{0:T(128)S(1)} %fusion.37), kind=kLoop, calls=%fused_computation.33 | loop fusion | flops 460800 | bytes 2211968 | tf_op jit(solution)/shard_map/sub | solution.py:192
  (13 shorter events, 0.3 us)
Async XLA Ops:
  0.6 27.1 %copy-start.1 = (f32[4,180,720]{2,1,0:T(8,128)S(1)}, f32[4,180,720]{2,1,0:T(8,128)}, u32[]{:S(2)}) copy-start(f32[4,180,720]{2,1,0:T(8,128)} %constant.96) | copy-start | bytes 6220804
  0.6 27.1 %copy-start.3 = (f32[720]{0:T(1024)S(1)}, f32[720]{0:T(1024)}, u32[]{:S(2)}) copy-start(f32[720]{0:T(1024)} %constant.93.clone) | copy-start | bytes 8644
  0.7 27.1 %copy-start.4 = (s32[720]{0:T(1024)S(1)}, s32[720]{0:T(1024)}, u32[]{:S(2)}) copy-start(s32[720]{0:T(1024)} %constant.94.clone) | copy-start | bytes 8644
  0.7 26.1 %copy-start.5 = (s32[256]{0:T(256)S(1)}, s32[256]{0:T(256)}, u32[]{:S(2)}) copy-start(s32[256]{0:T(256)} %param.8) | copy-start | bytes 3076
  3.5 45.1 %collective-permute-start.1 = (f32[4,5,3,180]{3,2,1,0:T(4,128)}, f32[4,5,3,180]{3,2,1,0:T(4,128)}, u32[]{:S(2)}, u32[]{:S(2)}) collective-permute-start(f32[4,5,3,180]{3,2,1,0:T(4,128)} %get-tuple-element.7), channel_id=1, source_target_pairs={{4,0},{8,4},{12,8},{16,12},{20,16},{24,20},{28,24},{5,1},{9,5},{13... | collective-permute-start | bytes 129608 | tf_op jit(solution)/shard_map/ppermute | solution.py:20
  4.8 43.8 %collective-permute-start = (f32[4,5,3,180]{3,2,1,0:T(4,128)}, f32[4,5,3,180]{3,2,1,0:T(4,128)S(1)}, u32[]{:S(2)}, u32[]{:S(2)}) collective-permute-start(f32[4,5,3,180]{3,2,1,0:T(4,128)} %get-tuple-element.6), channel_id=1, source_target_pairs={{0,4},{4,8},{8,12},{12,16},{16,20},{20,24},{24,28},{1,5},{5,9},{9,... | collective-permute-start | bytes 129608 | tf_op jit(solution)/shard_map/ppermute | solution.py:18
  27.7 2.2 %copy-start.2 = (f32[128,180]{0,1:T(8,128)S(1)}, f32[128,180]{0,1:T(8,128)}, u32[]{:S(2)}) copy-start(f32[128,180]{0,1:T(8,128)} %copy.30) | copy-start | bytes 276484
  29.9 16.2 %copy-start = (f32[4,4,32,180]{3,2,1,0:T(8,128)S(1)}, f32[4,4,32,180]{3,2,1,0:T(8,128)}, u32[]{:S(2)}) copy-start(f32[4,4,32,180]{3,2,1,0:T(8,128)} %param.6) | copy-start | bytes 1105924

commit v3 on v2

--- a/solution.py
+++ b/solution.py
@@ -146,17 +146,36 @@
     flat_count = levels * lat_rows
     flat_zonal = zonal.reshape(flat_count, lon_cols)
     edges = jnp.concatenate([tracers[..., :3], tracers[..., lon_cols - 3 :]], axis=-1)
-    gathered = lax.all_gather(flat_zonal, "lon", axis=0)
-    gathered_edges = lax.all_gather(edges, "lon", axis=0)
     west_index = (lon_index + lon_groups - 1) % lon_groups
     east_index = (lon_index + 1) % lon_groups
-    west = lax.dynamic_index_in_dim(gathered_edges, west_index, 0, keepdims=False)[..., 3:]
-    east = lax.dynamic_index_in_dim(gathered_edges, east_index, 0, keepdims=False)[..., :3]
+    if lon_groups <= 8:
+        edge_rows = jnp.transpose(edges, (0, 2, 1, 3)).reshape(flat_count, tracer_count * 6)
+        payload = jnp.concatenate([flat_zonal, edge_rows], axis=1)
+        received = [payload] + [
+            lax.ppermute(payload, "lon", [(i, (i + s) % lon_groups) for i in range(lon_groups)])
+            for s in range(1, lon_groups)
+        ]
+        stacked = jnp.stack([part[:, :lon_cols] for part in received], axis=0)
+        order = (lon_index - jnp.arange(lon_groups, dtype=jnp.int32)) % lon_groups
+        gathered = jnp.take(stacked, order, axis=0)
+
+        def edge_block(part):
+            block = part[:, lon_cols:].reshape(levels, lat_rows, tracer_count, 6)
+            return jnp.transpose(block, (0, 2, 1, 3))
+
+        west = edge_block(received[1 % lon_groups])[..., 3:]
+        east = edge_block(received[(lon_groups - 1) % lon_groups])[..., :3]
+        west_raw = received[1 % lon_groups][:, lon_cols - 1 : lon_cols]
+    else:
+        gathered = lax.all_gather(flat_zonal, "lon", axis=0)
+        gathered_edges = lax.all_gather(edges, "lon", axis=0)
+        west = lax.dynamic_index_in_dim(gathered_edges, west_index, 0, keepdims=False)[..., 3:]
+        east = lax.dynamic_index_in_dim(gathered_edges, east_index, 0, keepdims=False)[..., :3]
+        west_raw = lax.dynamic_index_in_dim(gathered, west_index, 0, keepdims=False)[:, -1:]
     lon_ext = jnp.concatenate([west, tracers, east], axis=-1)
     local_limits = lax.dynamic_slice_in_dim(cutoffs, band_index * lat_rows, lat_rows)
     limits = jnp.tile(local_limits, levels)
     circle = lon_cols * lon_groups
-    west_raw = lax.dynamic_index_in_dim(gathered, west_index, 0, keepdims=False)[:, -1:]
     raw_ext = jnp.concatenate([west_raw, flat_zonal], axis=1)
     if circle <= 2048:
         table, scale, wavenumber = dense_tables(circle)

time: 52.8 us -> 38 us (0.72)
  the two profiles are of different devices: /device:TPU:0 before, /device:TPU:12 now
where the time goes in v3:
time: 38 us; the launch traced here: 37.5 us
  local copies, waits for them, and re-layouts  12.5 us (33%)
  starting transfers between devices  10.7 us (28%)
  other arithmetic  6.63 us (17%)
  matrix products  4.67 us (12%)
  waiting for transfers between devices  2.06 us (5%)
  between operations  0.92 us (2%)
    ppermute x3, starting transfers between devices, body(): lax.ppermute(payload, 'lon', [(i, (i + s) % lon_groups) for i in range(lo...  6.41 us
    another operation x4, local copies, waits for them, and re-layouts, body(): stacked = jnp.stack([part[:, :lon_cols] for part in received], axis=0)  3.59 us
    dot_general x1, matrix products, body(): jnp.einsum('prm,pmw->rw', gathered, table[1:].reshape(lon_groups, lon_col...  3.21 us
    ppermute x1, starting transfers between devices, padded(): lax.ppermute(tail, axis, [(i, (i + 1) % count) for i in range(ends)])  2.39 us
    gather x1, local copies, waits for them, and re-layouts, body(): gathered = jnp.take(stacked, order, axis=0)  2.3 us
    ppermute x1, waiting for transfers between devices, padded(): lax.ppermute(tail, axis, [(i, (i + 1) % count) for i in range(ends)])  2.05 us
    ppermute x1, starting transfers between devices, padded(): lax.ppermute(head, axis, [((i + 1) % count, i) for i in range(ends)])  1.94 us
    dot_general x1, matrix products, body(): lowpass_ext = jnp.einsum('rw,nw->rn', coeff, local_table, precision=high)  1.46 us
  transfers between devices with their start and end apart: 5, of which 1 were waited for; matrix products, arithmetic and copies ran while one was open for 14% of the time, Pallas kernels for 0%

profile of v3, /device:TPU:12, one launch (start us, length us, event | category | flops | bytes accessed | tf_op | source)
XLA Modules:
  0.0 37.5 jit_solution(5413914620257630947)
XLA Ops:
  0.6 0.0 copy-start
  0.7 1.0 %fusion.48 = (f32[1,4,32,180]{3,2,1,0:T(8,128)S(1)}, f32[4,1,32,180]{3,2,1,0:T(8,128)S(1)}) fusion(f32[2,4,32,180]{3,2,1,0:T(8,128)} %param.7), kind=kLoop, calls=%fused_computation.100 | loop fusion | bytes 368640 | tf_op jit(solution)/shard_map/slice | solution.py:142
  1.7 1.2 %fusion.47 = (f32[4,4,32,3]{3,2,1,0:T(8,128)S(1)}, f32[4,4,32,3]{3,2,1,0:T(8,128)S(1)}) fusion(f32[4,4,32,180]{3,2,1,0:T(8,128)} %param.6), kind=kLoop, calls=%fused_computation.99 | loop fusion | bytes 24576 | tf_op jit(solution)/shard_map/slice | solution.py:148
  2.9 0.2 copy.38
  3.0 0.2 copy.37
  3.3 0.1 reshape.132
  3.4 0.1 copy.30
  3.5 0.7 %pad_maximum_fusion.8 = f32[128,204]{0,1:T(8,128)} fusion(f32[128,24]{0,1:T(8,128)S(1)} %reshape.132, f32[128,180]{0,1:T(8,128)S(1)} %copy.30), kind=kLoop, calls=%fused_computation.67 | loop fusion | flops 26112 | bytes 208896 | tf_op jit(solution)/shard_map/concatenate | solution.py:153
  4.1 0.4 %collective-permute-start.2 = (f32[128,204]{0,1:T(8,128)}, f32[128,204]{0,1:T(8,128)}, u32[]{:S(2)}, u32[]{:S(2)}) collective-permute-start(f32[128,204]{0,1:T(8,128)} %pad_maximum_fusion.8), channel_id=1, source_target_pairs={{0,3},{1,0},{2,1},{3,2},{4,7},{5,4},{6,5},{7,6},{8,11},{9,8},{10,9... | collective-permute-start | bytes 313352 | tf_op jit(solution)/shard_map/ppermute | solution.py:155
  4.6 1.6 %collective-permute-start = (f32[128,204]{0,1:T(8,128)}, f32[128,204]{0,1:T(8,128)}, u32[]{:S(2)}, u32[]{:S(2)}) collective-permute-start(f32[128,204]{0,1:T(8,128)} %pad_maximum_fusion.8), channel_id=1, source_target_pairs={{0,1},{1,2},{2,3},{3,0},{4,5},{5,6},{6,7},{7,4},{8,9},{9,10},{10,1... | collective-permute-start | bytes 313352 | tf_op jit(solution)/shard_map/ppermute | solution.py:155
  6.2 4.4 %collective-permute-start.1 = (f32[128,204]{0,1:T(8,128)}, f32[128,204]{0,1:T(8,128)}, u32[]{:S(2)}, u32[]{:S(2)}) collective-permute-start(f32[128,204]{0,1:T(8,128)} %pad_maximum_fusion.8), channel_id=1, source_target_pairs={{0,2},{1,3},{2,0},{3,1},{4,6},{5,7},{6,4},{7,5},{8,10},{9,11},{10,... | collective-permute-start | bytes 313352 | tf_op jit(solution)/shard_map/ppermute | solution.py:155
  10.6 1.9 %collective-permute-start.4 = (f32[4,5,3,180]{3,2,1,0:T(4,128)S(1)}, f32[4,5,3,180]{3,2,1,0:T(4,128)S(1)}, u32[]{:S(2)}, u32[]{:S(2)}) collective-permute-start(f32[4,5,3,180]{3,2,1,0:T(4,128)S(1)} %get-tuple-element.7), channel_id=1, source_target_pairs={{4,0},{8,4},{12,8},{16,12},{20,16},{24,20},{28,24},{5,1},{9,5},{13... | collective-permute-start | bytes 129608 | tf_op jit(solution)/shard_map/ppermute | solution.py:20
  12.5 2.4 %collective-permute-start.3 = (f32[4,5,3,180]{3,2,1,0:T(4,128)S(1)}, f32[4,5,3,180]{3,2,1,0:T(4,128)S(1)}, u32[]{:S(2)}, u32[]{:S(2)}) collective-permute-start(f32[4,5,3,180]{3,2,1,0:T(4,128)S(1)} %get-tuple-element.6), channel_id=1, source_target_pairs={{0,4},{4,8},{8,12},{12,16},{16,20},{20,24},{24,28},{1,5},{5,9},{9,... | collective-permute-start | bytes 129608 | tf_op jit(solution)/shard_map/ppermute | solution.py:18
  14.9 0.6 %compare_and_fusion = pred[4]{0:T(512)(128)(4,1)} fusion(s32[]{:T(128)S(6)} %axis_index.25), kind=kLoop, calls=%fused_computation.85 | loop fusion | flops 72 | bytes 8 | tf_op jit(solution)/shard_map/jit(_take)/and | solution.py:160
  15.6 0.1 dynamic_slice.6
  15.7 0.1 tile.10
  15.8 0.6 %fusion.39 = f32[32]{0:T(128)} fusion(s32[]{:T(128)S(6)} %mul.206), kind=kLoop, calls=%fused_computation.91 | loop fusion | flops 192 | bytes 132 | tf_op jit(solution)/shard_map/sin | solution.py:62
  16.4 0.7 %copy.31 = f32[1,128,180]{1,2,0:T(8,128)} copy(f32[1,128,180]{2,1,0:T(8,128)S(1)} %bitcast.52) | data formatting | bytes 184320 | tf_op jit(solution)/shard_map/stack;reshape;squeeze | solution.py:158
  17.1 2.0 %collective-permute-done.3 = f32[4,5,3,180]{3,2,1,0:T(4,128)S(1)} collective-permute-done((f32[4,5,3,180]{3,2,1,0:T(4,128)S(1)}, f32[4,5,3,180]{3,2,1,0:T(4,128)S(1)}, u32[]{:S(2)}, u32[]{:S(2)}) %collective-permute-start.3) | collective-permute-done | bytes 43232 | tf_op jit(solution)/shard_map/ppermute | solution.py:18
  19.2 0.1 pad_maximum_fusion
  19.3 0.3 fusion.14
  19.6 0.2 slice_subtract_fusion
  19.9 0.4 %fusion.7 = f32[4,4,33,180]{3,2,1,0:T(8,128)S(1)} fusion(f32[4,4,34,180]{3,2,1,0:T(8,128)S(1)} %get-tuple-element.5, f32[4,4,34,180]{3,2,1,0:T(8,128)S(1)} %get-tuple-element.4, f32[4,4,35,180]{3,2,1,0:T(8,128)S(1)} %fusion.14, f32[33]{0:T(128)S(1)} %multiply_sine_fusion, f32[4,33,180]{2,1,0:T(8,128)S(1)} %get-tuple-element.16, ...), kind=kLoop, calls=%fused_computation.11 | loop fusion | flops 1045440 | bytes 2685012 | tf_op jit(solution)/shard_map/mul | solution.py:203
  20.3 0.0 copy-start.1
  20.4 0.0 copy-start.3
  20.4 0.0 copy-start.4
  20.4 1.0 %slice_bitcast_fusion.2 = f32[1,128,180]{1,2,0:T(8,128)S(1)} fusion(f32[128,204]{0,1:T(8,128)} %collective-permute-done.2), kind=kLoop, calls=%fused_computation.68 | loop fusion | bytes 184320 | tf_op jit(solution)/shard_map/stack | solution.py:158
  21.4 0.9 %slice_bitcast_fusion.3 = f32[1,128,180]{1,2,0:T(8,128)S(1)} fusion(f32[128,204]{0,1:T(8,128)} %collective-permute-done.1), kind=kLoop, calls=%fused_computation.69 | loop fusion | bytes 184320 | tf_op jit(solution)/shard_map/stack | solution.py:158
  22.4 0.9 %slice_bitcast_fusion.4 = f32[1,128,180]{1,2,0:T(8,128)S(1)} fusion(f32[128,204]{0,1:T(8,128)} %collective-permute-done), kind=kLoop, calls=%fused_computation.70 | loop fusion | bytes 184320 | tf_op jit(solution)/shard_map/stack | solution.py:158
  23.3 0.8 %pad_maximum_fusion.6 = f32[4,128,180]{1,2,0:T(8,128)} fusion(f32[1,128,180]{1,2,0:T(8,128)S(1)} %slice_bitcast_fusion.2, f32[1,128,180]{1,2,0:T(8,128)S(1)} %slice_bitcast_fusion.3, f32[1,128,180]{1,2,0:T(8,128)S(1)} %slice_bitcast_fusion.4, f32[1,128,180]{1,2,0:T(8,128)S(1)} %copy-done.2), kind=kLoop, calls=%fused_computation.54 | loop fusion | flops 276480 | bytes 737280 | tf_op jit(solution)/shard_map/stack | solution.py:158
  24.0 2.3 %gather_fusion = f32[4,128,180]{1,2,0:T(8,128)} fusion(f32[4,128,180]{1,2,0:T(8,128)} %pad_maximum_fusion.6, s32[1024]{0:T(1024)S(1)} %pad_clamp_fusion), kind=kCustom, calls=%fused_computation | custom fusion | bytes 737296 | tf_op jit(solution)/shard_map/jit(_take)/gather | solution.py:160
  26.4 3.2 %fusion.1 = f32[128,720]{0,1:T(8,128)S(1)} fusion(f32[4,180,720]{2,1,0:T(8,128)S(1)} %copy-done.1, f32[4,128,180]{1,2,0:T(8,128)} %gather_fusion, pred[4]{0:T(512)(128)(4,1)} %compare_and_fusion, f32[720]{0:T(1024)S(1)} %copy-done.3, s32[128]{0:T(128)S(1)} %tile.10, s32[720]{0:T(1024)S(1)} %copy-done.4), kind=kOutput, calls=%fused_computation.3 | convolution fusion | flops 398499840 | bytes 2817156 | tf_op jit(solution)/shard_map/prm,pmw->rw/dot_general | solution.py:183
  29.6 0.7 %slice.196 = f32[128,1]{0,1:T(1,128)S(1)} slice(f32[128,204]{0,1:T(8,128)} %collective-permute-done), slice={[0:128], [179:180]} | slice | bytes 1024 | tf_op jit(solution)/shard_map/slice | solution.py:168
  30.2 1.5 %maximum_select_fusion = f32[128,181]{0,1:T(8,128)S(1)} fusion(f32[128,180]{0,1:T(8,128)S(1)} %copy.30, f32[128,1]{0,1:T(1,128)S(1)} %slice.196, pred[128]{0:T(512)(128)(4,1)S(1)} %broadcast_compare_fusion.1, f32[128,720]{0,1:T(8,128)S(1)} %fusion.1, f32[721,720]{1,0:T(8,128)} %constant.92.clone, s32[]{:T(128)S(6)} %select_n.67), kind=kOutput, calls=%fused_computation.71 | convolution fusion | flops 100132096 | bytes 1119364 | tf_op jit(solution)/shard_map/rw,nw->rn/dot_general | solution.py:191
  31.7 0.1 copy.33
  31.9 0.7 %slice.199 = f32[128,24]{0,1:T(8,128)S(1)} slice(f32[128,204]{0,1:T(8,128)} %collective-permute-done.2), slice={[0:128], [180:204]} | slice | bytes 24576 | tf_op jit(solution)/shard_map/slice | solution.py:163
  32.6 0.1 reshape.135
  32.7 0.2 copy.35
  32.9 0.7 %slice.197 = f32[128,24]{0,1:T(8,128)S(1)} slice(f32[128,204]{0,1:T(8,128)} %collective-permute-done), slice={[0:128], [180:204]} | slice | bytes 24576 | tf_op jit(solution)/shard_map/slice | solution.py:163
  33.6 0.1 reshape.134
  33.7 0.2 copy.34
  33.9 0.1 slice.198
  34.0 0.3 pad_maximum_fusion.5
  34.3 0.5 %fusion.31 = f32[4,4,32,183]{3,2,1,0:T(8,128)S(1)} fusion(f32[4,4,32,186]{3,2,1,0:T(8,128)S(1)} %pad_maximum_fusion.5, f32[4,4,32,180]{3,2,1,0:T(8,128)S(1)} %copy-done, f32[4,4,32,3]{3,2,1,0:T(8,128)S(1)} %slice.198, f32[4,4,32,3]{3,2,1,0:T(8,128)S(1)} %bitcast.49), kind=kLoop, calls=%fused_computation.49 | loop fusion | flops 655872 | bytes 1505280 | tf_op jit(solution)/shard_map/sub | solution.py:33
  34.8 0.3 slice_subtract_fusion.3
  35.2 0.8 %slice_bitcast_fusion = f32[4,32,180]{2,1,0:T(8,128)} fusion(f32[4,1,32,181]{3,2,0,1:T(8,128)S(1)} %bitcast.46), kind=kLoop, calls=%fused_computation.63 | loop fusion | bytes 184320 | tf_op jit(solution)/shard_map/squeeze | solution.py:199
  35.9 0.5 %fusion.25 = f32[4,4,32,181]{3,2,1,0:T(8,128)S(1)} fusion(f32[4,4,32,182]{3,2,1,0:T(8,128)S(1)} %get-tuple-element.9, f32[4,4,32,182]{3,2,1,0:T(8,128)S(1)} %get-tuple-element.8, f32[4,4,32,183]{3,2,1,0:T(8,128)S(1)} %fusion.31, f32[4,32,181]{2,1,0:T(8,128)S(1)} %get-tuple-element.18, f32[4,32,181]{2,1,0:T(8,128)S(1)} %get-tuple-element.19, ...), kind=kLoop, calls=%fused_computation.40 | loop fusion | flops 926720 | bytes 2617984 | tf_op jit(solution)/shard_map/mul | solution.py:53
  36.5 1.0 %fusion.20 = f32[4,4,32,180]{3,2,1,0:T(8,128)} fusion(f32[4,4,32,180]{3,2,1,0:T(8,128)S(1)} %copy-done, f32[4,4,33,180]{3,2,1,0:T(8,128)S(1)} %fusion.7, f32[4,4,32,181]{3,2,1,0:T(8,128)S(1)} %fusion.25, f32[32]{0:T(128)S(1)} %copy-done.5), kind=kLoop, calls=%fused_computation.33 | loop fusion | flops 460800 | bytes 2211968 | tf_op jit(solution)/shard_map/sub | solution.py:211
  (26 shorter events, 0.3 us)
Async XLA Ops:
  0.6 9.9 %copy-start = (f32[4,4,32,180]{3,2,1,0:T(8,128)S(1)}, f32[4,4,32,180]{3,2,1,0:T(8,128)}, u32[]{:S(2)}) copy-start(f32[4,4,32,180]{3,2,1,0:T(8,128)} %param.6) | copy-start | bytes 1105924
  0.6 14.9 %copy-start.6 = (s32[256]{0:T(256)S(1)}, s32[256]{0:T(256)}, u32[]{:S(2)}) copy-start(s32[256]{0:T(256)} %param.8) | copy-start | bytes 3076
  4.1 16.3 %collective-permute-start.2 = (f32[128,204]{0,1:T(8,128)}, f32[128,204]{0,1:T(8,128)}, u32[]{:S(2)}, u32[]{:S(2)}) collective-permute-start(f32[128,204]{0,1:T(8,128)} %pad_maximum_fusion.8), channel_id=1, source_target_pairs={{0,3},{1,0},{2,1},{3,2},{4,7},{5,4},{6,5},{7,6},{8,11},{9,8},{10,9... | collective-permute-start | bytes 313352 | tf_op jit(solution)/shard_map/ppermute | solution.py:155
  4.6 17.8 %collective-permute-start = (f32[128,204]{0,1:T(8,128)}, f32[128,204]{0,1:T(8,128)}, u32[]{:S(2)}, u32[]{:S(2)}) collective-permute-start(f32[128,204]{0,1:T(8,128)} %pad_maximum_fusion.8), channel_id=1, source_target_pairs={{0,1},{1,2},{2,3},{3,0},{4,5},{5,6},{6,7},{7,4},{8,9},{9,10},{10,1... | collective-permute-start | bytes 313352 | tf_op jit(solution)/shard_map/ppermute | solution.py:155
  6.2 15.3 %collective-permute-start.1 = (f32[128,204]{0,1:T(8,128)}, f32[128,204]{0,1:T(8,128)}, u32[]{:S(2)}, u32[]{:S(2)}) collective-permute-start(f32[128,204]{0,1:T(8,128)} %pad_maximum_fusion.8), channel_id=1, source_target_pairs={{0,2},{1,3},{2,0},{3,1},{4,6},{5,7},{6,4},{7,5},{8,10},{9,11},{10,... | collective-permute-start | bytes 313352 | tf_op jit(solution)/shard_map/ppermute | solution.py:155
  10.6 6.6 %collective-permute-start.4 = (f32[4,5,3,180]{3,2,1,0:T(4,128)S(1)}, f32[4,5,3,180]{3,2,1,0:T(4,128)S(1)}, u32[]{:S(2)}, u32[]{:S(2)}) collective-permute-start(f32[4,5,3,180]{3,2,1,0:T(4,128)S(1)} %get-tuple-element.7), channel_id=1, source_target_pairs={{4,0},{8,4},{12,8},{16,12},{20,16},{24,20},{28,24},{5,1},{9,5},{13... | collective-permute-start | bytes 129608 | tf_op jit(solution)/shard_map/ppermute | solution.py:20
  12.5 6.7 %collective-permute-start.3 = (f32[4,5,3,180]{3,2,1,0:T(4,128)S(1)}, f32[4,5,3,180]{3,2,1,0:T(4,128)S(1)}, u32[]{:S(2)}, u32[]{:S(2)}) collective-permute-start(f32[4,5,3,180]{3,2,1,0:T(4,128)S(1)} %get-tuple-element.6), channel_id=1, source_target_pairs={{0,4},{4,8},{8,12},{12,16},{16,20},{20,24},{24,28},{1,5},{5,9},{9,... | collective-permute-start | bytes 129608 | tf_op jit(solution)/shard_map/ppermute | solution.py:18
  19.9 3.4 %copy-start.2 = (f32[1,128,180]{1,2,0:T(8,128)S(1)}, f32[1,128,180]{1,2,0:T(8,128)}, u32[]{:S(2)}) copy-start(f32[1,128,180]{1,2,0:T(8,128)} %copy.31) | copy-start | bytes 276484
  20.3 6.0 %copy-start.1 = (f32[4,180,720]{2,1,0:T(8,128)S(1)}, f32[4,180,720]{2,1,0:T(8,128)}, u32[]{:S(2)}) copy-start(f32[4,180,720]{2,1,0:T(8,128)} %constant.96) | copy-start | bytes 6220804
  20.4 6.0 %copy-start.3 = (f32[720]{0:T(1024)S(1)}, f32[720]{0:T(1024)}, u32[]{:S(2)}) copy-start(f32[720]{0:T(1024)} %constant.93.clone) | copy-start | bytes 8644
  20.4 6.0 %copy-start.4 = (s32[720]{0:T(1024)S(1)}, s32[720]{0:T(1024)}, u32[]{:S(2)}) copy-start(s32[720]{0:T(1024)} %constant.94.clone) | copy-start | bytes 8644
  35.2 1.3 %copy-start.5 = (f32[32]{0:T(128)S(1)}, f32[32]{0:T(128)}, u32[]{:S(2)}) copy-start(f32[32]{0:T(128)} %fusion.39) | copy-start | bytes 388

commit v4 on v2

--- a/solution.py
+++ b/solution.py
@@ -125,11 +125,7 @@
     )
     wavenumber = np.concatenate([cos_ids, sin_ids])
     scale = np.where((wavenumber == 0) | (wavenumber == half), 1.0, 2.0) / circle
-    return (
-        jnp.asarray(table.astype(np.float32)),
-        jnp.asarray(scale.astype(np.float32)),
-        jnp.asarray(wavenumber.astype(np.int32)),
-    )
+    return (table, scale, wavenumber)
 
 
 def body(tracers, courant, cutoffs):
@@ -146,35 +142,53 @@
     flat_count = levels * lat_rows
     flat_zonal = zonal.reshape(flat_count, lon_cols)
     edges = jnp.concatenate([tracers[..., :3], tracers[..., lon_cols - 3 :]], axis=-1)
-    gathered = lax.all_gather(flat_zonal, "lon", axis=0)
-    gathered_edges = lax.all_gather(edges, "lon", axis=0)
     west_index = (lon_index + lon_groups - 1) % lon_groups
     east_index = (lon_index + 1) % lon_groups
-    west = lax.dynamic_index_in_dim(gathered_edges, west_index, 0, keepdims=False)[..., 3:]
-    east = lax.dynamic_index_in_dim(gathered_edges, east_index, 0, keepdims=False)[..., :3]
-    lon_ext = jnp.concatenate([west, tracers, east], axis=-1)
     local_limits = lax.dynamic_slice_in_dim(cutoffs, band_index * lat_rows, lat_rows)
     limits = jnp.tile(local_limits, levels)
     circle = lon_cols * lon_groups
-    west_raw = lax.dynamic_index_in_dim(gathered, west_index, 0, keepdims=False)[:, -1:]
-    raw_ext = jnp.concatenate([west_raw, flat_zonal], axis=1)
-    if circle <= 2048:
+    if lon_groups <= 8 and circle <= 2048:
+        edge_rows = jnp.transpose(edges, (0, 2, 1, 3)).reshape(flat_count, tracer_count * 6)
+        payload = jnp.concatenate([flat_zonal, edge_rows], axis=1)
+        received = [payload] + [
+            lax.ppermute(payload, "lon", [(i, (i - s) % lon_groups) for i in range(lon_groups)])
+            for s in range(1, lon_groups)
+        ]
+
+        def edge_block(part):
+            block = part[:, lon_cols:].reshape(levels, lat_rows, tracer_count, 6)
+            return jnp.transpose(block, (0, 2, 1, 3))
+
+        east_part = received[1 % lon_groups]
+        west_part = received[(lon_groups - 1) % lon_groups]
+        west = edge_block(west_part)[..., 3:]
+        east = edge_block(east_part)[..., :3]
+        raw_ext = jnp.concatenate([west_part[:, lon_cols - 1 : lon_cols], flat_zonal], axis=1)
         table, scale, wavenumber = dense_tables(circle)
+        width = payload.shape[1]
+        forward = np.zeros((lon_groups, width, circle), np.float32)
+        forward[:, :lon_cols, :] = table[1:].reshape(lon_groups, lon_cols, circle)
+        forward = jnp.asarray(forward)
+        inverse_rows = jnp.asarray(table[: lon_cols + 1].astype(np.float32))
         high = lax.Precision.HIGH
-        coeff = jnp.einsum(
-            "prm,pmw->rw",
-            gathered,
-            table[1:].reshape(lon_groups, lon_cols, circle),
-            precision=high,
-        )
-        coeff = jnp.where(wavenumber[None, :] <= limits[:, None], coeff * scale[None, :], 0.0)
-        local_table = lax.dynamic_slice_in_dim(table, lon_index * lon_cols, lon_cols + 1, axis=0)
-        lowpass_ext = jnp.einsum("rw,nw->rn", coeff, local_table, precision=high)
+        coeff = jnp.dot(received[0], forward[0], precision=high)
+        for s in range(1, lon_groups):
+            coeff = coeff + jnp.dot(received[s], forward[s], precision=high)
+        keep = jnp.asarray(wavenumber.astype(np.int32))[None, :] <= limits[:, None]
+        coeff = jnp.where(keep, coeff * jnp.asarray(scale.astype(np.float32))[None, :], 0.0)
+        lowpass_ext = jnp.einsum("rw,nw->rn", coeff, inverse_rows, precision=high)
     else:
+        gathered = lax.all_gather(flat_zonal, "lon", axis=0)
+        gathered_edges = lax.all_gather(edges, "lon", axis=0)
+        west = lax.dynamic_index_in_dim(gathered_edges, west_index, 0, keepdims=False)[..., 3:]
+        east = lax.dynamic_index_in_dim(gathered_edges, east_index, 0, keepdims=False)[..., :3]
+        west_raw = lax.dynamic_index_in_dim(gathered, west_index, 0, keepdims=False)[:, -1:]
+        raw_ext = jnp.concatenate([west_raw, flat_zonal], axis=1)
         whole_rows = jnp.transpose(gathered, (1, 0, 2)).reshape(flat_count, circle)
         lowpass = spectral_lowpass(whole_rows, limits, lon_groups)
         lowpass = jnp.concatenate([lowpass[:, -1:], lowpass], axis=1)
         lowpass_ext = lax.dynamic_slice_in_dim(lowpass, lon_index * lon_cols, lon_cols + 1, axis=1)
+    lon_ext = jnp.concatenate([west, tracers, east], axis=-1)
     filtered_flat = jnp.where((limits < circle // 2)[:, None], lowpass_ext, raw_ext)
     zonal_faces = filtered_flat.reshape(levels, 1, lat_rows, lon_cols + 1)
     filtered_zonal = zonal_faces[:, 0, :, 1:]

time: 52.8 us -> 27.2 us (0.52)
  the two profiles are of different devices: /device:TPU:0 before, /device:TPU:12 now
where the time goes in v4:
time: 27.2 us; the launch traced here: 27 us
  starting transfers between devices  10.8 us (40%)
  local copies, waits for them, and re-layouts  5.06 us (19%)
  other arithmetic  4 us (15%)
  matrix products  3.92 us (14%)
  waiting for transfers between devices  2.21 us (8%)
  between operations  0.99 us (4%)
    ppermute x3, starting transfers between devices, body(): lax.ppermute(payload, 'lon', [(i, (i - s) % lon_groups) for i in range(lo...  6.47 us
    dot_general x3, matrix products, body(): coeff = coeff + jnp.dot(received[s], forward[s], precision=high)  2.43 us
    ppermute x1, starting transfers between devices, padded(): lax.ppermute(tail, axis, [(i, (i + 1) % count) for i in range(ends)])  2.39 us
    ppermute x1, waiting for transfers between devices, padded(): lax.ppermute(tail, axis, [(i, (i + 1) % count) for i in range(ends)])  2.2 us
    unnamed x20, local copies, waits for them, and re-layouts  1.99 us
    ppermute x1, starting transfers between devices, padded(): lax.ppermute(head, axis, [((i + 1) % count, i) for i in range(ends)])  1.94 us
    dot_general x2, matrix products, body(): coeff = jnp.dot(received[0], forward[0], precision=high)  1.09 us
    slice x1, local copies, waits for them, and re-layouts, body(): zonal = courant[0]  1.04 us
  transfers between devices with their start and end apart: 5, of which 1 were waited for; matrix products, arithmetic and copies ran while one was open for 15% of the time, Pallas kernels for 0%

profile of v4, /device:TPU:12, one launch (start us, length us, event | category | flops | bytes accessed | tf_op | source)
XLA Modules:
  0.0 27.0 jit_solution(16750900390734037154)
XLA Ops:
  0.6 1.0 %fusion.40 = (f32[1,4,32,180]{3,2,1,0:T(8,128)S(1)}, f32[4,1,32,180]{3,2,1,0:T(8,128)S(1)}) fusion(f32[2,4,32,180]{3,2,1,0:T(8,128)} %param.8), kind=kLoop, calls=%fused_computation.81 | loop fusion | bytes 368640 | tf_op jit(solution)/shard_map/slice | solution.py:138
  1.7 0.1 copy-done
  1.8 0.1 fusion.39
  1.9 0.2 copy.36
  2.1 0.2 copy.35
  2.3 0.1 reshape.75
  2.4 0.1 copy.29
  2.5 0.0 copy-start.5
  2.6 0.5 %collective-permute-start = (f32[128,204]{0,1:T(8,128)S(1)}, f32[128,204]{0,1:T(8,128)S(1)}, u32[]{:S(2)}, u32[]{:S(2)}) collective-permute-start(f32[128,204]{0,1:T(8,128)S(1)} %pad_maximum_fusion.7), channel_id=1, source_target_pairs={{0,3},{1,0},{2,1},{3,2},{4,7},{5,4},{6,5},{7,6},{8,11},{9,8},{10,9... | collective-permute-start | bytes 313352 | tf_op jit(solution)/shard_map/ppermute | solution.py:154
  3.1 1.6 %collective-permute-start.2 = (f32[128,204]{0,1:T(8,128)S(1)}, f32[128,204]{0,1:T(8,128)S(1)}, u32[]{:S(2)}, u32[]{:S(2)}) collective-permute-start(f32[128,204]{0,1:T(8,128)S(1)} %pad_maximum_fusion.7), channel_id=1, source_target_pairs={{0,1},{1,2},{2,3},{3,0},{4,5},{5,6},{6,7},{7,4},{8,9},{9,10},{10,1... | collective-permute-start | bytes 313352 | tf_op jit(solution)/shard_map/ppermute | solution.py:154
  4.6 4.4 %collective-permute-start.1 = (f32[128,204]{0,1:T(8,128)S(1)}, f32[128,204]{0,1:T(8,128)S(1)}, u32[]{:S(2)}, u32[]{:S(2)}) collective-permute-start(f32[128,204]{0,1:T(8,128)S(1)} %pad_maximum_fusion.7), channel_id=1, source_target_pairs={{0,2},{1,3},{2,0},{3,1},{4,6},{5,7},{6,4},{7,5},{8,10},{9,11},{10,... | collective-permute-start | bytes 313352 | tf_op jit(solution)/shard_map/ppermute | solution.py:154
  9.1 1.9 %collective-permute-start.4 = (f32[4,5,3,180]{3,2,1,0:T(4,128)S(1)}, f32[4,5,3,180]{3,2,1,0:T(4,128)S(1)}, u32[]{:S(2)}, u32[]{:S(2)}) collective-permute-start(f32[4,5,3,180]{3,2,1,0:T(4,128)S(1)} %get-tuple-element.7), channel_id=1, source_target_pairs={{4,0},{8,4},{12,8},{16,12},{20,16},{24,20},{28,24},{5,1},{9,5},{13... | collective-permute-start | bytes 129608 | tf_op jit(solution)/shard_map/ppermute | solution.py:20
  11.0 2.4 %collective-permute-start.3 = (f32[4,5,3,180]{3,2,1,0:T(4,128)S(1)}, f32[4,5,3,180]{3,2,1,0:T(4,128)S(1)}, u32[]{:S(2)}, u32[]{:S(2)}) collective-permute-start(f32[4,5,3,180]{3,2,1,0:T(4,128)S(1)} %get-tuple-element.6), channel_id=1, source_target_pairs={{0,4},{4,8},{8,12},{12,16},{16,20},{20,24},{24,28},{1,5},{5,9},{9,... | collective-permute-start | bytes 129608 | tf_op jit(solution)/shard_map/ppermute | solution.py:18
  13.5 0.0 copy-start.8
  13.5 0.7 %copy-done.8 = s32[256]{0:T(256)S(1)} copy-done((s32[256]{0:T(256)S(1)}, s32[256]{0:T(256)}, u32[]{:S(2)}) %copy-start.8) | copy-done | bytes 1048
  14.1 0.1 dynamic_slice.3
  14.2 0.1 tile.10
  14.3 0.8 %convolution_bitcast_fusion = f32[128,720]{0,1:T(8,128)S(1)} fusion(f32[180,720]{1,0:T(8,128)S(1)} %copy-done.5, f32[128,180]{1,0:T(8,128)S(1)} %bitcast.48), kind=kOutput, calls=%fused_computation.1 | convolution fusion | flops 99532800 | bytes 979200 | tf_op jit(solution)/shard_map/dot_general | solution.py:174
  15.1 0.3 %convolution_add_fusion = f32[128,720]{0,1:T(8,128)S(1)} fusion(f32[128,720]{0,1:T(8,128)S(1)} %convolution_bitcast_fusion, f32[128,24]{0,1:T(8,128)S(1)} %reshape.75), kind=kOutput, calls=%fused_computation | convolution fusion | flops 13363200 | bytes 749568 | tf_op jit(solution)/shard_map/dot_general | solution.py:174
  15.5 2.2 %collective-permute-done.3 = f32[4,5,3,180]{3,2,1,0:T(4,128)S(1)} collective-permute-done((f32[4,5,3,180]{3,2,1,0:T(4,128)S(1)}, f32[4,5,3,180]{3,2,1,0:T(4,128)S(1)}, u32[]{:S(2)}, u32[]{:S(2)}) %collective-permute-start.3) | collective-permute-done | bytes 43232 | tf_op jit(solution)/shard_map/ppermute | solution.py:18
  17.7 0.1 pad_maximum_fusion
  17.8 0.3 fusion.16
  18.1 0.2 slice_subtract_fusion
  18.4 0.0 copy-start.3
  18.4 0.4 %fusion.9 = f32[4,4,33,180]{3,2,1,0:T(8,128)S(1)} fusion(f32[4,4,34,180]{3,2,1,0:T(8,128)S(1)} %get-tuple-element.5, f32[4,4,34,180]{3,2,1,0:T(8,128)S(1)} %get-tuple-element.4, f32[4,4,35,180]{3,2,1,0:T(8,128)S(1)} %fusion.16, f32[33]{0:T(128)S(1)} %multiply_sine_fusion, f32[4,33,180]{2,1,0:T(8,128)S(1)} %get-tuple-element.16, ...), kind=kLoop, calls=%fused_computation.14 | loop fusion | flops 1045440 | bytes 2685012 | tf_op jit(solution)/shard_map/mul | solution.py:198
  18.8 0.0 copy-start.2
  18.8 0.6 %copy-done.3 = f32[204,720]{1,0:T(8,128)S(1)} copy-done((f32[204,720]{1,0:T(8,128)S(1)}, f32[204,720]{1,0:T(8,128)}, u32[]{:S(2)}) %copy-start.3) | copy-done | bytes 587544
  19.5 0.8 %fusion.42 = f32[128,720]{0,1:T(8,128)S(1)} fusion(f32[128,204]{0,1:T(8,128)S(1)} %collective-permute-done.2, f32[204,720]{1,0:T(8,128)S(1)} %copy-done.3), kind=kOutput, calls=%fused_computation.83 | convolution fusion | flops 112803840 | bytes 1060608 | tf_op jit(solution)/shard_map/dot_general | solution.py:176
  20.2 0.0 copy-start.1
  20.3 0.0 copy-start.6
  20.3 0.0 copy-start.7
  20.3 0.8 %fusion.41 = f32[128,720]{0,1:T(8,128)S(1)} fusion(f32[128,204]{0,1:T(8,128)S(1)} %collective-permute-done.1, f32[204,720]{1,0:T(8,128)S(1)} %copy-done.2), kind=kOutput, calls=%fused_computation.82 | convolution fusion | flops 112803840 | bytes 1060608 | tf_op jit(solution)/shard_map/dot_general | solution.py:176
  21.1 0.0 copy-start.4
  21.1 0.2 copy-done.1
  21.3 0.9 %fusion.3 = f32[128,720]{0,1:T(8,128)S(1)} fusion(f32[128,720]{0,1:T(8,128)S(1)} %fusion.42, f32[128,720]{0,1:T(8,128)S(1)} %fusion.41, f32[128,720]{0,1:T(8,128)S(1)} %convolution_add_fusion, f32[128,204]{0,1:T(8,128)S(1)} %collective-permute-done, f32[204,720]{1,0:T(8,128)S(1)} %copy-done.1, f32[720]{0:T(1024)S(1)} %copy-done.6, s32[128]{0:T(128)S(1)} %tile.10, ...), kind=kOutput, calls=%fused_computation.6 | convolution fusion | flops 113356800 | bytes 2172800 | tf_op jit(solution)/shard_map/dot_general | solution.py:176
  22.2 0.4 %maximum_select_fusion = f32[128,181]{0,1:T(8,128)S(1)} fusion(f32[128,180]{0,1:T(8,128)S(1)} %copy.29, f32[128,1]{0,1:T(1,128)S(1)} %slice.193, pred[128]{0:T(512)(128)(4,1)S(1)} %broadcast_compare_fusion.1, f32[128,720]{0,1:T(8,128)S(1)} %fusion.3, f32[181,720]{1,0:T(8,128)S(1)} %copy-done.4), kind=kOutput, calls=%fused_computation.65 | convolution fusion | flops 100132096 | bytes 1075392 | tf_op jit(solution)/shard_map/rw,nw->rn/dot_general | solution.py:179
  22.6 0.1 copy.31
  22.8 0.1 reshape.77
  22.9 0.2 copy.33
  23.1 0.1 reshape.76
  23.2 0.2 copy.32
  23.4 0.1 slice.195
  23.5 0.3 %pad_maximum_fusion.5 = f32[4,4,32,186]{3,2,1,0:T(8,128)S(1)} fusion(f32[4,4,32,3]{3,2,1,0:T(8,128)S(1)} %bitcast.44, f32[4,4,32,180]{3,2,1,0:T(8,128)S(1)} %copy-done, f32[4,4,32,3]{3,2,1,0:T(8,128)S(1)} %slice.195), kind=kLoop, calls=%fused_computation.51 | loop fusion | flops 190464 | bytes 761856 | tf_op jit(solution)/shard_map/concatenate | solution.py:191
  23.8 0.6 %fusion.31 = f32[4,4,32,183]{3,2,1,0:T(8,128)S(1)} fusion(f32[4,4,32,186]{3,2,1,0:T(8,128)S(1)} %pad_maximum_fusion.5, f32[4,4,32,180]{3,2,1,0:T(8,128)S(1)} %copy-done, f32[4,4,32,3]{3,2,1,0:T(8,128)S(1)} %slice.195, f32[4,4,32,3]{3,2,1,0:T(8,128)S(1)} %bitcast.45), kind=kLoop, calls=%fused_computation.50 | loop fusion | flops 655872 | bytes 1505280 | tf_op jit(solution)/shard_map/sub | solution.py:33
  24.3 0.3 %slice_subtract_fusion.3 = (f32[4,4,32,182]{3,2,1,0:T(8,128)S(1)}, f32[4,4,32,182]{3,2,1,0:T(8,128)S(1)}) fusion(f32[4,4,32,183]{3,2,1,0:T(8,128)S(1)} %fusion.31, f32[4,4,32,186]{3,2,1,0:T(8,128)S(1)} %pad_maximum_fusion.5), kind=kLoop, calls=%fused_computation.54 | loop fusion | flops 465920 | bytes 1863680 | tf_op jit(solution)/shard_map/sub | solution.py:43
  24.7 0.8 %slice_bitcast_fusion = f32[4,32,180]{2,1,0:T(8,128)} fusion(f32[4,1,32,181]{3,2,0,1:T(8,128)S(1)} %bitcast.42), kind=kLoop, calls=%fused_computation.60 | loop fusion | bytes 184320 | tf_op jit(solution)/shard_map/squeeze | solution.py:194
  25.4 0.5 %fusion.25 = f32[4,4,32,181]{3,2,1,0:T(8,128)S(1)} fusion(f32[4,4,32,182]{3,2,1,0:T(8,128)S(1)} %get-tuple-element.9, f32[4,4,32,182]{3,2,1,0:T(8,128)S(1)} %get-tuple-element.8, f32[4,4,32,183]{3,2,1,0:T(8,128)S(1)} %fusion.31, f32[4,32,181]{2,1,0:T(8,128)S(1)} %get-tuple-element.18, f32[4,32,181]{2,1,0:T(8,128)S(1)} %get-tuple-element.19, ...), kind=kLoop, calls=%fused_computation.41 | loop fusion | flops 926720 | bytes 2617984 | tf_op jit(solution)/shard_map/mul | solution.py:53
  25.9 1.0 %fusion.20 = f32[4,4,32,180]{3,2,1,0:T(8,128)} fusion(f32[4,4,32,180]{3,2,1,0:T(8,128)S(1)} %copy-done, f32[4,4,33,180]{3,2,1,0:T(8,128)S(1)} %fusion.9, f32[4,4,32,181]{3,2,1,0:T(8,128)S(1)} %fusion.25, f32[32]{0:T(128)S(1)} %fusion.37), kind=kLoop, calls=%fused_computation.34 | loop fusion | flops 460800 | bytes 2211968 | tf_op jit(solution)/shard_map/sub | solution.py:206
  (25 shorter events, 0.4 us)
Async XLA Ops:
  0.6 1.2 %copy-start = (f32[4,4,32,180]{3,2,1,0:T(8,128)S(1)}, f32[4,4,32,180]{3,2,1,0:T(8,128)}, u32[]{:S(2)}) copy-start(f32[4,4,32,180]{3,2,1,0:T(8,128)} %param.7) | copy-start | bytes 1105924
  2.5 11.8 %copy-start.5 = (f32[180,720]{1,0:T(8,128)S(1)}, f32[180,720]{1,0:T(8,128)}, u32[]{:S(2)}) copy-start(f32[180,720]{1,0:T(8,128)} %constant.70) | copy-start | bytes 1555204
  2.6 18.5 %collective-permute-start = (f32[128,204]{0,1:T(8,128)S(1)}, f32[128,204]{0,1:T(8,128)S(1)}, u32[]{:S(2)}, u32[]{:S(2)}) collective-permute-start(f32[128,204]{0,1:T(8,128)S(1)} %pad_maximum_fusion.7), channel_id=1, source_target_pairs={{0,3},{1,0},{2,1},{3,2},{4,7},{5,4},{6,5},{7,6},{8,11},{9,8},{10,9... | collective-permute-start | bytes 313352 | tf_op jit(solution)/shard_map/ppermute | solution.py:154
  3.1 15.8 %collective-permute-start.2 = (f32[128,204]{0,1:T(8,128)S(1)}, f32[128,204]{0,1:T(8,128)S(1)}, u32[]{:S(2)}, u32[]{:S(2)}) collective-permute-start(f32[128,204]{0,1:T(8,128)S(1)} %pad_maximum_fusion.7), channel_id=1, source_target_pairs={{0,1},{1,2},{2,3},{3,0},{4,5},{5,6},{6,7},{7,4},{8,9},{9,10},{10,1... | collective-permute-start | bytes 313352 | tf_op jit(solution)/shard_map/ppermute | solution.py:154
  4.6 15.6 %collective-permute-start.1 = (f32[128,204]{0,1:T(8,128)S(1)}, f32[128,204]{0,1:T(8,128)S(1)}, u32[]{:S(2)}, u32[]{:S(2)}) collective-permute-start(f32[128,204]{0,1:T(8,128)S(1)} %pad_maximum_fusion.7), channel_id=1, source_target_pairs={{0,2},{1,3},{2,0},{3,1},{4,6},{5,7},{6,4},{7,5},{8,10},{9,11},{10,... | collective-permute-start | bytes 313352 | tf_op jit(solution)/shard_map/ppermute | solution.py:154
  9.1 6.4 %collective-permute-start.4 = (f32[4,5,3,180]{3,2,1,0:T(4,128)S(1)}, f32[4,5,3,180]{3,2,1,0:T(4,128)S(1)}, u32[]{:S(2)}, u32[]{:S(2)}) collective-permute-start(f32[4,5,3,180]{3,2,1,0:T(4,128)S(1)} %get-tuple-element.7), channel_id=1, source_target_pairs={{4,0},{8,4},{12,8},{16,12},{20,16},{24,20},{28,24},{5,1},{9,5},{13... | collective-permute-start | bytes 129608 | tf_op jit(solution)/shard_map/ppermute | solution.py:20
  11.0 6.7 %collective-permute-start.3 = (f32[4,5,3,180]{3,2,1,0:T(4,128)S(1)}, f32[4,5,3,180]{3,2,1,0:T(4,128)S(1)}, u32[]{:S(2)}, u32[]{:S(2)}) collective-permute-start(f32[4,5,3,180]{3,2,1,0:T(4,128)S(1)} %get-tuple-element.6), channel_id=1, source_target_pairs={{0,4},{4,8},{8,12},{12,16},{16,20},{20,24},{24,28},{1,5},{5,9},{9,... | collective-permute-start | bytes 129608 | tf_op jit(solution)/shard_map/ppermute | solution.py:18
  13.5 0.7 %copy-start.8 = (s32[256]{0:T(256)S(1)}, s32[256]{0:T(256)}, u32[]{:S(2)}) copy-start(s32[256]{0:T(256)} %param.9) | copy-start | bytes 3076
  18.4 1.1 %copy-start.3 = (f32[204,720]{1,0:T(8,128)S(1)}, f32[204,720]{1,0:T(8,128)}, u32[]{:S(2)}) copy-start(f32[204,720]{1,0:T(8,128)} %constant.69) | copy-start | bytes 1762564
  18.8 1.4 %copy-start.2 = (f32[204,720]{1,0:T(8,128)S(1)}, f32[204,720]{1,0:T(8,128)}, u32[]{:S(2)}) copy-start(f32[204,720]{1,0:T(8,128)} %constant.21) | copy-start | bytes 1762564
  20.2 1.1 %copy-start.1 = (f32[204,720]{1,0:T(8,128)S(1)}, f32[204,720]{1,0:T(8,128)}, u32[]{:S(2)}) copy-start(f32[204,720]{1,0:T(8,128)} %constant.19) | copy-start | bytes 1762564
  20.3 1.1 %copy-start.6 = (f32[720]{0:T(1024)S(1)}, f32[720]{0:T(1024)}, u32[]{:S(2)}) copy-start(f32[720]{0:T(1024)} %constant.15.clone) | copy-start | bytes 8644
  20.3 1.0 %copy-start.7 = (s32[720]{0:T(1024)S(1)}, s32[720]{0:T(1024)}, u32[]{:S(2)}) copy-start(s32[720]{0:T(1024)} %constant.14.clone) | copy-start | bytes 8644
  21.1 1.1 %copy-start.4 = (f32[181,720]{1,0:T(8,128)S(1)}, f32[181,720]{1,0:T(8,128)}, u32[]{:S(2)}) copy-start(f32[181,720]{1,0:T(8,128)} %constant.13.clone) | copy-start | bytes 1563844

commit v5 on v4

--- a/solution.py
+++ b/solution.py
@@ -138,7 +138,6 @@
     zonal = courant[0]
     meridional = courant[1]
     lat_stack = jnp.concatenate([tracers, meridional[:, None]], axis=1)
-    lat_ext = padded(lat_stack, (("lat", 2),), 3, False)
     flat_count = levels * lat_rows
     flat_zonal = zonal.reshape(flat_count, lon_cols)
     edges = jnp.concatenate([tracers[..., :3], tracers[..., lon_cols - 3 :]], axis=-1)
@@ -154,6 +153,9 @@
             lax.ppermute(payload, "lon", [(i, (i - s) % lon_groups) for i in range(lon_groups)])
             for s in range(1, lon_groups)
         ]
+
+        lat_stack, received = lax.optimization_barrier((lat_stack, received))
+        lat_ext = padded(lat_stack, (("lat", 2),), 3, False)
 
         def edge_block(part):
             block = part[:, lon_cols:].reshape(levels, lat_rows, tracer_count, 6)
@@ -178,6 +180,7 @@
         coeff = jnp.where(keep, coeff * jnp.asarray(scale.astype(np.float32))[None, :], 0.0)
         lowpass_ext = jnp.einsum("rw,nw->rn", coeff, inverse_rows, precision=high)
     else:
+        lat_ext = padded(lat_stack, (("lat", 2),), 3, False)
         gathered = lax.all_gather(flat_zonal, "lon", axis=0)
         gathered_edges = lax.all_gather(edges, "lon", axis=0)
         west = lax.dynamic_index_in_dim(gathered_edges, west_index, 0, keepdims=False)[..., 3:]

time: 27.2 us -> 32.3 us (1.19)
  the two profiles are of different devices: /device:TPU:12 before, /device:TPU:1 now
where the time goes in v5:
time: 32.3 us; the launch traced here: 32 us
  starting transfers between devices  10.7 us (33%)
  waiting for transfers between devices  7.88 us (24%)
  local copies, waits for them, and re-layouts  4.87 us (15%)
  other arithmetic  4.01 us (12%)
  matrix products  3.61 us (11%)
  between operations  0.92 us (3%)
    ppermute x3, waiting for transfers between devices, body(): lax.ppermute(payload, 'lon', [(i, (i - s) % lon_groups) for i in range(lo...  7.87 us
    ppermute x3, starting transfers between devices, body(): lax.ppermute(payload, 'lon', [(i, (i - s) % lon_groups) for i in range(lo...  4.65 us
    ppermute x1, starting transfers between devices, padded(): lax.ppermute(tail, axis, [(i, (i + 1) % count) for i in range(ends)])  3.02 us
    ppermute x1, starting transfers between devices, padded(): lax.ppermute(head, axis, [((i + 1) % count, i) for i in range(ends)])  3.01 us
    dot_general x3, matrix products, body(): coeff = coeff + jnp.dot(received[s], forward[s], precision=high)  2.32 us
    unnamed x20, local copies, waits for them, and re-layouts  1.77 us
    slice x1, local copies, waits for them, and re-layouts, body(): zonal = courant[0]  1.04 us
    sub x1, other arithmetic, body(): return (tracers - change, filtered_zonal)  1.03 us
  transfers between devices with their start and end apart: 5, of which 2 were waited for; matrix products, arithmetic and copies ran while one was open for 11% of the time, Pallas kernels for 0%

profile of v5, /device:TPU:1, one launch (start us, length us, event | category | flops | bytes accessed | tf_op | source)
XLA Modules:
  0.0 32.0 jit_solution(1115899579943537221)
XLA Ops:
  0.6 1.0 %fusion.39 = (f32[1,4,32,180]{3,2,1,0:T(8,128)S(1)}, f32[4,1,32,180]{3,2,1,0:T(8,128)S(1)}) fusion(f32[2,4,32,180]{3,2,1,0:T(8,128)} %param.8), kind=kLoop, calls=%fused_computation.75 | loop fusion | bytes 368640 | tf_op jit(solution)/shard_map/slice | solution.py:138
  1.7 0.1 copy-done
  1.8 0.1 fusion.38
  1.9 0.2 copy.36
  2.1 0.2 copy.35
  2.3 0.1 reshape.75
  2.4 0.1 copy.29
  2.6 4.2 %collective-permute-start = (f32[128,204]{0,1:T(8,128)S(1)}, f32[128,204]{0,1:T(8,128)S(1)}, u32[]{:S(2)}, u32[]{:S(2)}) collective-permute-start(f32[128,204]{0,1:T(8,128)S(1)} %pad_maximum_fusion.6), channel_id=1, source_target_pairs={{0,3},{1,0},{2,1},{3,2},{4,7},{5,4},{6,5},{7,6},{8,11},{9,8},{10,9... | collective-permute-start | bytes 313352 | tf_op jit(solution)/shard_map/ppermute | solution.py:153
  6.7 0.0 collective-permute-start.1
  6.7 0.5 %collective-permute-start.2 = (f32[128,204]{0,1:T(8,128)S(1)}, f32[128,204]{0,1:T(8,128)S(1)}, u32[]{:S(2)}, u32[]{:S(2)}) collective-permute-start(f32[128,204]{0,1:T(8,128)S(1)} %pad_maximum_fusion.6), channel_id=1, source_target_pairs={{0,1},{1,2},{2,3},{3,0},{4,5},{5,6},{6,7},{7,4},{8,9},{9,10},{10,1... | collective-permute-start | bytes 313352 | tf_op jit(solution)/shard_map/ppermute | solution.py:153
  7.2 0.1 pad_maximum_fusion.3
  7.3 0.0 copy-start.3
  7.3 0.6 %copy-done.8 = s32[256]{0:T(256)S(1)} copy-done((s32[256]{0:T(256)S(1)}, s32[256]{0:T(256)}, u32[]{:S(2)}) %copy-start.8) | copy-done | bytes 1048
  7.9 0.1 dynamic_slice.3
  8.0 0.1 tile.10
  8.1 0.4 %collective-permute-done = f32[128,204]{0,1:T(8,128)S(1)} collective-permute-done((f32[128,204]{0,1:T(8,128)S(1)}, f32[128,204]{0,1:T(8,128)S(1)}, u32[]{:S(2)}, u32[]{:S(2)}) %collective-permute-start) | collective-permute-done | bytes 104480 | tf_op jit(solution)/shard_map/ppermute | solution.py:153
  8.5 7.5 %collective-permute-done.1 = f32[128,204]{0,1:T(8,128)S(1)} collective-permute-done((f32[128,204]{0,1:T(8,128)S(1)}, f32[128,204]{0,1:T(8,128)S(1)}, u32[]{:S(2)}, u32[]{:S(2)}) %collective-permute-start.1) | collective-permute-done | bytes 104480 | tf_op jit(solution)/shard_map/ppermute | solution.py:153
  16.0 0.0 collective-permute-done.2
  16.0 0.8 %fusion.42 = f32[128,720]{0,1:T(8,128)S(1)} fusion(f32[128,204]{0,1:T(8,128)S(1)} %collective-permute-done.2, f32[204,720]{1,0:T(8,128)S(1)} %copy-done.4), kind=kOutput, calls=%fused_computation.78 | convolution fusion | flops 112803840 | bytes 1060608 | tf_op jit(solution)/shard_map/dot_general | solution.py:178
  16.8 0.0 copy-done.3
  16.8 0.0 copy-start.2
  16.8 0.8 %fusion.40 = f32[128,720]{0,1:T(8,128)S(1)} fusion(f32[128,204]{0,1:T(8,128)S(1)} %collective-permute-done, f32[204,720]{1,0:T(8,128)S(1)} %copy-done.3), kind=kOutput, calls=%fused_computation.76 | convolution fusion | flops 112803840 | bytes 1060608 | tf_op jit(solution)/shard_map/dot_general | solution.py:178
  17.6 0.3 copy-done.2
  17.9 0.8 %fusion.41 = f32[128,720]{0,1:T(8,128)S(1)} fusion(f32[128,204]{0,1:T(8,128)S(1)} %collective-permute-done.1, f32[204,720]{1,0:T(8,128)S(1)} %copy-done.2), kind=kOutput, calls=%fused_computation.77 | convolution fusion | flops 112803840 | bytes 1060608 | tf_op jit(solution)/shard_map/dot_general | solution.py:178
  18.7 0.3 copy-done.1
  19.0 0.9 %fusion.3 = f32[128,720]{0,1:T(8,128)S(1)} fusion(f32[128,720]{0,1:T(8,128)S(1)} %fusion.42, f32[128,720]{0,1:T(8,128)S(1)} %fusion.41, f32[128,720]{0,1:T(8,128)S(1)} %fusion.40, f32[128,204]{0,1:T(8,128)S(1)} %pad_maximum_fusion.6, f32[204,720]{1,0:T(8,128)S(1)} %copy-done.1, f32[720]{0:T(1024)S(1)} %copy-done.6, s32[128]{0:T(128)S(1)} %tile.10, ...), kind=kOutput, calls=%fused_computation.4 | convolution fusion | flops 113356800 | bytes 2172800 | tf_op jit(solution)/shard_map/dot_general | solution.py:176
  19.9 0.2 copy-done.5
  20.0 0.4 %convolution_select_fusion = f32[128,181]{0,1:T(8,128)S(1)} fusion(f32[128,720]{0,1:T(8,128)S(1)} %fusion.3, f32[181,720]{1,0:T(8,128)S(1)} %copy-done.5, f32[128,180]{0,1:T(8,128)S(1)} %copy.29, f32[128,1]{0,1:T(1,128)S(1)} %slice.156, pred[128]{0:T(512)(128)(4,1)S(1)} %broadcast_compare_fusion.1), kind=kOutput, calls=%fused_computation.5 | convolution fusion | flops 100132096 | bytes 1075392 | tf_op jit(solution)/shard_map/rw,nw->rn/dot_general | solution.py:181
  20.4 0.1 copy.31
  20.7 3.0 %collective-permute-start.4 = (f32[4,5,3,180]{3,2,1,0:T(4,128)S(1)}, f32[4,5,3,180]{3,2,1,0:T(4,128)S(1)}, u32[]{:S(2)}, u32[]{:S(2)}) collective-permute-start(f32[4,5,3,180]{3,2,1,0:T(4,128)S(1)} %get-tuple-element.17), channel_id=1, source_target_pairs={{4,0},{8,4},{12,8},{16,12},{20,16},{24,20},{28,24},{5,1},{9,5},{13... | collective-permute-start | bytes 129608 | tf_op jit(solution)/shard_map/ppermute | solution.py:20
  23.7 3.0 %collective-permute-start.3 = (f32[4,5,3,180]{3,2,1,0:T(4,128)S(1)}, f32[4,5,3,180]{3,2,1,0:T(4,128)S(1)}, u32[]{:S(2)}, u32[]{:S(2)}) collective-permute-start(f32[4,5,3,180]{3,2,1,0:T(4,128)S(1)} %get-tuple-element.16), channel_id=1, source_target_pairs={{0,4},{4,8},{8,12},{12,16},{16,20},{20,24},{24,28},{1,5},{5,9},{9,... | collective-permute-start | bytes 129608 | tf_op jit(solution)/shard_map/ppermute | solution.py:18
  26.7 0.1 reshape.77
  26.8 0.2 copy.33
  27.0 0.1 reshape.76
  27.1 0.2 copy.32
  27.2 0.1 slice.191
  27.4 0.3 pad_maximum_fusion.4
  27.7 0.6 %fusion.31 = f32[4,4,32,183]{3,2,1,0:T(8,128)S(1)} fusion(f32[4,4,32,186]{3,2,1,0:T(8,128)S(1)} %pad_maximum_fusion.4, f32[4,4,32,180]{3,2,1,0:T(8,128)S(1)} %copy-done, f32[4,4,32,3]{3,2,1,0:T(8,128)S(1)} %slice.191, f32[4,4,32,3]{3,2,1,0:T(8,128)S(1)} %bitcast.42), kind=kLoop, calls=%fused_computation.48 | loop fusion | flops 655872 | bytes 1505280 | tf_op jit(solution)/shard_map/sub | solution.py:33
  28.2 0.3 %slice_subtract_fusion.3 = (f32[4,4,32,182]{3,2,1,0:T(8,128)S(1)}, f32[4,4,32,182]{3,2,1,0:T(8,128)S(1)}) fusion(f32[4,4,32,183]{3,2,1,0:T(8,128)S(1)} %fusion.31, f32[4,4,32,186]{3,2,1,0:T(8,128)S(1)} %pad_maximum_fusion.4), kind=kLoop, calls=%fused_computation.52 | loop fusion | flops 465920 | bytes 1863680 | tf_op jit(solution)/shard_map/sub | solution.py:43
  28.6 0.5 %fusion.25 = f32[4,4,32,181]{3,2,1,0:T(8,128)S(1)} fusion(f32[4,4,32,182]{3,2,1,0:T(8,128)S(1)} %get-tuple-element.19, f32[4,4,32,182]{3,2,1,0:T(8,128)S(1)} %get-tuple-element.18, f32[4,4,32,183]{3,2,1,0:T(8,128)S(1)} %fusion.31, f32[4,32,181]{2,1,0:T(8,128)S(1)} %get-tuple-element.28, f32[4,32,181]{2,1,0:T(8,128)S(1)} %get-tuple-element.29, ...), kind=kLoop, calls=%fused_computation.39 | loop fusion | flops 926720 | bytes 2617984 | tf_op jit(solution)/shard_map/mul | solution.py:53
  29.1 0.8 %slice_bitcast_fusion = f32[4,32,180]{2,1,0:T(8,128)} fusion(f32[4,1,32,181]{3,2,0,1:T(8,128)S(1)} %bitcast.40), kind=kLoop, calls=%fused_computation.58 | loop fusion | bytes 184320 | tf_op jit(solution)/shard_map/squeeze | solution.py:197
  29.8 0.0 collective-permute-done.4
  29.8 0.0 collective-permute-done.3
  29.8 0.1 pad_maximum_fusion
  29.9 0.3 fusion.16
  30.2 0.2 slice_subtract_fusion
  30.5 0.4 %fusion.9 = f32[4,4,33,180]{3,2,1,0:T(8,128)S(1)} fusion(f32[4,4,34,180]{3,2,1,0:T(8,128)S(1)} %get-tuple-element.15, f32[4,4,34,180]{3,2,1,0:T(8,128)S(1)} %get-tuple-element.14, f32[4,4,35,180]{3,2,1,0:T(8,128)S(1)} %fusion.16, f32[33]{0:T(128)S(1)} %multiply_sine_fusion, f32[4,33,180]{2,1,0:T(8,128)S(1)} %get-tuple-element.26, ...), kind=kLoop, calls=%fused_computation.13 | loop fusion | flops 1045440 | bytes 2685012 | tf_op jit(solution)/shard_map/mul | solution.py:201
  30.9 1.0 %fusion.20 = f32[4,4,32,180]{3,2,1,0:T(8,128)} fusion(f32[4,4,32,180]{3,2,1,0:T(8,128)S(1)} %copy-done, f32[4,4,33,180]{3,2,1,0:T(8,128)S(1)} %fusion.9, f32[4,4,32,181]{3,2,1,0:T(8,128)S(1)} %fusion.25, f32[32]{0:T(128)S(1)} %fusion.36), kind=kLoop, calls=%fused_computation.32 | loop fusion | flops 460800 | bytes 2211968 | tf_op jit(solution)/shard_map/sub | solution.py:209
  (25 shorter events, 0.4 us)
Async XLA Ops:
  0.6 1.2 %copy-start = (f32[4,4,32,180]{3,2,1,0:T(8,128)S(1)}, f32[4,4,32,180]{3,2,1,0:T(8,128)}, u32[]{:S(2)}) copy-start(f32[4,4,32,180]{3,2,1,0:T(8,128)} %param.7) | copy-start | bytes 1105924
  2.6 5.9 %collective-permute-start = (f32[128,204]{0,1:T(8,128)S(1)}, f32[128,204]{0,1:T(8,128)S(1)}, u32[]{:S(2)}, u32[]{:S(2)}) collective-permute-start(f32[128,204]{0,1:T(8,128)S(1)} %pad_maximum_fusion.6), channel_id=1, source_target_pairs={{0,3},{1,0},{2,1},{3,2},{4,7},{5,4},{6,5},{7,6},{8,11},{9,8},{10,9... | collective-permute-start | bytes 313352 | tf_op jit(solution)/shard_map/ppermute | solution.py:153
  6.7 9.2 %collective-permute-start.1 = (f32[128,204]{0,1:T(8,128)S(1)}, f32[128,204]{0,1:T(8,128)S(1)}, u32[]{:S(2)}, u32[]{:S(2)}) collective-permute-start(f32[128,204]{0,1:T(8,128)S(1)} %pad_maximum_fusion.6), channel_id=1, source_target_pairs={{0,2},{1,3},{2,0},{3,1},{4,6},{5,7},{6,4},{7,5},{8,10},{9,11},{10,... | collective-permute-start | bytes 313352 | tf_op jit(solution)/shard_map/ppermute | solution.py:153
  6.7 9.2 %collective-permute-start.2 = (f32[128,204]{0,1:T(8,128)S(1)}, f32[128,204]{0,1:T(8,128)S(1)}, u32[]{:S(2)}, u32[]{:S(2)}) collective-permute-start(f32[128,204]{0,1:T(8,128)S(1)} %pad_maximum_fusion.6), channel_id=1, source_target_pairs={{0,1},{1,2},{2,3},{3,0},{4,5},{5,6},{6,7},{7,4},{8,9},{9,10},{10,1... | collective-permute-start | bytes 313352 | tf_op jit(solution)/shard_map/ppermute | solution.py:153
  7.2 0.7 %copy-start.8 = (s32[256]{0:T(256)S(1)}, s32[256]{0:T(256)}, u32[]{:S(2)}) copy-start(s32[256]{0:T(256)} %param.9) | copy-start | bytes 3076
  7.2 8.8 %copy-start.4 = (f32[204,720]{1,0:T(8,128)S(1)}, f32[204,720]{1,0:T(8,128)}, u32[]{:S(2)}) copy-start(f32[204,720]{1,0:T(8,128)} %constant.69) | copy-start | bytes 1762564
  7.3 9.5 %copy-start.3 = (f32[204,720]{1,0:T(8,128)S(1)}, f32[204,720]{1,0:T(8,128)}, u32[]{:S(2)}) copy-start(f32[204,720]{1,0:T(8,128)} %constant.19) | copy-start | bytes 1762564
  16.8 1.1 %copy-start.2 = (f32[204,720]{1,0:T(8,128)S(1)}, f32[204,720]{1,0:T(8,128)}, u32[]{:S(2)}) copy-start(f32[204,720]{1,0:T(8,128)} %constant.21) | copy-start | bytes 1762564
  17.9 1.1 %copy-start.1 = (f32[204,720]{1,0:T(8,128)S(1)}, f32[204,720]{1,0:T(8,128)}, u32[]{:S(2)}) copy-start(f32[204,720]{1,0:T(8,128)} %constant.17) | copy-start | bytes 1762564
  17.9 1.1 %copy-start.6 = (f32[720]{0:T(1024)S(1)}, f32[720]{0:T(1024)}, u32[]{:S(2)}) copy-start(f32[720]{0:T(1024)} %constant.15.clone) | copy-start | bytes 8644
  17.9 1.1 %copy-start.7 = (s32[720]{0:T(1024)S(1)}, s32[720]{0:T(1024)}, u32[]{:S(2)}) copy-start(s32[720]{0:T(1024)} %constant.14.clone) | copy-start | bytes 8644
  19.0 1.1 %copy-start.5 = (f32[181,720]{1,0:T(8,128)S(1)}, f32[181,720]{1,0:T(8,128)}, u32[]{:S(2)}) copy-start(f32[181,720]{1,0:T(8,128)} %constant.13.clone) | copy-start | bytes 1563844
  20.7 9.2 %collective-permute-start.4 = (f32[4,5,3,180]{3,2,1,0:T(4,128)S(1)}, f32[4,5,3,180]{3,2,1,0:T(4,128)S(1)}, u32[]{:S(2)}, u32[]{:S(2)}) collective-permute-start(f32[4,5,3,180]{3,2,1,0:T(4,128)S(1)} %get-tuple-element.17), channel_id=1, source_target_pairs={{4,0},{8,4},{12,8},{16,12},{20,16},{24,20},{28,24},{5,1},{9,5},{13... | collective-permute-start | bytes 129608 | tf_op jit(solution)/shard_map/ppermute | solution.py:20
  23.7 6.2 %collective-permute-start.3 = (f32[4,5,3,180]{3,2,1,0:T(4,128)S(1)}, f32[4,5,3,180]{3,2,1,0:T(4,128)S(1)}, u32[]{:S(2)}, u32[]{:S(2)}) collective-permute-start(f32[4,5,3,180]{3,2,1,0:T(4,128)S(1)} %get-tuple-element.16), channel_id=1, source_target_pairs={{0,4},{4,8},{8,12},{12,16},{16,20},{20,24},{24,28},{1,5},{5,9},{9,... | collective-permute-start | bytes 129608 | tf_op jit(solution)/shard_map/ppermute | solution.py:18

commit v6 on v4

--- a/solution.py
+++ b/solution.py
@@ -137,8 +137,16 @@
     grid_rows = lat_rows * lat_bands
     zonal = courant[0]
     meridional = courant[1]
-    lat_stack = jnp.concatenate([tracers, meridional[:, None]], axis=1)
-    lat_ext = padded(lat_stack, (("lat", 2),), 3, False)
+    lat_count = lax.axis_size("lat")
+    lat_head = jnp.concatenate([tracers[:, :, :3], meridional[:, None, :3]], axis=1)
+    lat_tail = jnp.concatenate(
+        [tracers[:, :, lat_rows - 3 :], meridional[:, None, lat_rows - 3 :]], axis=1
+    )
+    from_north = lax.ppermute(lat_tail, "lat", [(i, i + 1) for i in range(lat_count - 1)])
+    from_south = lax.ppermute(lat_head, "lat", [(i + 1, i) for i in range(lat_count - 1)])
+    lat_ext = jnp.concatenate(
+        [from_north, jnp.concatenate([tracers, meridional[:, None]], axis=1), from_south], axis=2
+    )
     flat_count = levels * lat_rows
     flat_zonal = zonal.reshape(flat_count, lon_cols)
     edges = jnp.concatenate([tracers[..., :3], tracers[..., lon_cols - 3 :]], axis=-1)

time: 27.2 us -> 27.3 us (level)
  no operation moved by 1% of the time
where the time goes in v6:
time: 27.3 us; the launch traced here: 27 us
  starting transfers between devices  10.8 us (40%)
  local copies, waits for them, and re-layouts  5.09 us (19%)
  other arithmetic  4.02 us (15%)
  matrix products  3.93 us (14%)
  waiting for transfers between devices  2.2 us (8%)
  between operations  1 us (4%)
    ppermute x3, starting transfers between devices, body(): lax.ppermute(payload, 'lon', [(i, (i - s) % lon_groups) for i in range(lo...  6.47 us
    dot_general x3, matrix products, body(): coeff = coeff + jnp.dot(received[s], forward[s], precision=high)  2.43 us
    ppermute x1, starting transfers between devices, body(): lax.ppermute(lat_tail, 'lat', [(i, i + 1) for i in range(lat_count - 1)])  2.39 us
    ppermute x1, waiting for transfers between devices, body(): lax.ppermute(lat_tail, 'lat', [(i, i + 1) for i in range(lat_count - 1)])  2.19 us
    unnamed x20, local copies, waits for them, and re-layouts  1.98 us
    ppermute x1, starting transfers between devices, body(): lax.ppermute(lat_head, 'lat', [(i + 1, i) for i in range(lat_count - 1)])  1.94 us
    dot_general x2, matrix products, body(): coeff = jnp.dot(received[0], forward[0], precision=high)  1.09 us
    slice x1, local copies, waits for them, and re-layouts, body(): zonal = courant[0]  1.05 us
  transfers between devices with their start and end apart: 5, of which 1 were waited for; matrix products, arithmetic and copies ran while one was open for 15% of the time, Pallas kernels for 0%

profile of v6, /device:TPU:12, one launch (start us, length us, event | category | flops | bytes accessed | tf_op | source)
XLA Modules:
  0.0 27.0 jit_solution(8178357862875016812)
XLA Ops:
  0.6 1.1 %fusion.41 = (f32[1,4,32,180]{3,2,1,0:T(8,128)S(1)}, f32[4,1,32,180]{3,2,1,0:T(8,128)S(1)}, f32[4,32,180]{2,1,0:T(8,128)S(1)}) fusion(f32[2,4,32,180]{3,2,1,0:T(8,128)} %param.8), kind=kLoop, calls=%fused_computation.85 | loop fusion | bytes 460800 | tf_op jit(solution)/shard_map/slice | solution.py:138
  1.7 0.1 copy-done
  1.8 0.1 fusion.39
  1.9 0.2 copy.42
  2.1 0.2 copy.41
  2.3 0.1 reshape.75
  2.4 0.1 copy.33
  2.6 0.5 %collective-permute-start = (f32[128,204]{0,1:T(8,128)S(1)}, f32[128,204]{0,1:T(8,128)S(1)}, u32[]{:S(2)}, u32[]{:S(2)}) collective-permute-start(f32[128,204]{0,1:T(8,128)S(1)} %pad_maximum_fusion.7), channel_id=1, source_target_pairs={{0,3},{1,0},{2,1},{3,2},{4,7},{5,4},{6,5},{7,6},{8,11},{9,8},{10,9... | collective-permute-start | bytes 313352 | tf_op jit(solution)/shard_map/ppermute | solution.py:162
  3.1 1.6 %collective-permute-start.2 = (f32[128,204]{0,1:T(8,128)S(1)}, f32[128,204]{0,1:T(8,128)S(1)}, u32[]{:S(2)}, u32[]{:S(2)}) collective-permute-start(f32[128,204]{0,1:T(8,128)S(1)} %pad_maximum_fusion.7), channel_id=1, source_target_pairs={{0,1},{1,2},{2,3},{3,0},{4,5},{5,6},{6,7},{7,4},{8,9},{9,10},{10,1... | collective-permute-start | bytes 313352 | tf_op jit(solution)/shard_map/ppermute | solution.py:162
  4.6 4.4 %collective-permute-start.1 = (f32[128,204]{0,1:T(8,128)S(1)}, f32[128,204]{0,1:T(8,128)S(1)}, u32[]{:S(2)}, u32[]{:S(2)}) collective-permute-start(f32[128,204]{0,1:T(8,128)S(1)} %pad_maximum_fusion.7), channel_id=1, source_target_pairs={{0,2},{1,3},{2,0},{3,1},{4,6},{5,7},{6,4},{7,5},{8,10},{9,11},{10,... | collective-permute-start | bytes 313352 | tf_op jit(solution)/shard_map/ppermute | solution.py:162
  9.1 1.9 %collective-permute-start.4 = (f32[4,5,3,180]{3,2,1,0:T(4,128)S(1)}, f32[4,5,3,180]{3,2,1,0:T(4,128)S(1)}, u32[]{:S(2)}, u32[]{:S(2)}) collective-permute-start(f32[4,5,3,180]{3,2,1,0:T(4,128)S(1)} %pad_maximum_fusion.9), channel_id=1, source_target_pairs={{4,0},{8,4},{12,8},{16,12},{20,16},{24,20},{28,24},{5,1},{9,5},{13... | collective-permute-start | bytes 129608 | tf_op jit(solution)/shard_map/ppermute | solution.py:146
  11.1 2.4 %collective-permute-start.3 = (f32[4,5,3,180]{3,2,1,0:T(4,128)S(1)}, f32[4,5,3,180]{3,2,1,0:T(4,128)S(1)}, u32[]{:S(2)}, u32[]{:S(2)}) collective-permute-start(f32[4,5,3,180]{3,2,1,0:T(4,128)S(1)} %pad_maximum_fusion.8), channel_id=1, source_target_pairs={{0,4},{4,8},{8,12},{12,16},{16,20},{20,24},{24,28},{1,5},{5,9},{9,... | collective-permute-start | bytes 129608 | tf_op jit(solution)/shard_map/ppermute | solution.py:145
  13.5 0.0 copy-start.8
  13.5 0.7 %copy-done.8 = s32[256]{0:T(256)S(1)} copy-done((s32[256]{0:T(256)S(1)}, s32[256]{0:T(256)}, u32[]{:S(2)}) %copy-start.8) | copy-done | bytes 1048
  14.2 0.1 dynamic_slice.3
  14.3 0.1 tile.10
  14.4 0.8 %convolution_bitcast_fusion = f32[128,720]{0,1:T(8,128)S(1)} fusion(f32[180,720]{1,0:T(8,128)S(1)} %copy-done.5, f32[128,180]{1,0:T(8,128)S(1)} %bitcast.58), kind=kOutput, calls=%fused_computation.1 | convolution fusion | flops 99532800 | bytes 979200 | tf_op jit(solution)/shard_map/dot_general | solution.py:182
  15.2 0.3 %convolution_add_fusion = f32[128,720]{0,1:T(8,128)S(1)} fusion(f32[128,720]{0,1:T(8,128)S(1)} %convolution_bitcast_fusion, f32[128,24]{0,1:T(8,128)S(1)} %reshape.75), kind=kOutput, calls=%fused_computation | convolution fusion | flops 13363200 | bytes 749568 | tf_op jit(solution)/shard_map/dot_general | solution.py:182
  15.5 2.2 %collective-permute-done.3 = f32[4,5,3,180]{3,2,1,0:T(4,128)S(1)} collective-permute-done((f32[4,5,3,180]{3,2,1,0:T(4,128)S(1)}, f32[4,5,3,180]{3,2,1,0:T(4,128)S(1)}, u32[]{:S(2)}, u32[]{:S(2)}) %collective-permute-start.3) | collective-permute-done | bytes 43232 | tf_op jit(solution)/shard_map/ppermute | solution.py:145
  17.7 0.1 pad_maximum_fusion
  17.9 0.3 fusion.16
  18.1 0.2 slice_subtract_fusion
  18.4 0.0 copy-start.3
  18.4 0.4 %fusion.9 = f32[4,4,33,180]{3,2,1,0:T(8,128)S(1)} fusion(f32[4,4,34,180]{3,2,1,0:T(8,128)S(1)} %get-tuple-element.5, f32[4,4,34,180]{3,2,1,0:T(8,128)S(1)} %get-tuple-element.4, f32[4,4,35,180]{3,2,1,0:T(8,128)S(1)} %fusion.16, f32[33]{0:T(128)S(1)} %multiply_sine_fusion, f32[4,33,180]{2,1,0:T(8,128)S(1)} %get-tuple-element.17, ...), kind=kLoop, calls=%fused_computation.14 | loop fusion | flops 1045440 | bytes 2685012 | tf_op jit(solution)/shard_map/mul | solution.py:206
  18.9 0.0 copy-start.2
  18.9 0.0 collective-permute-done.2
  18.9 0.6 %copy-done.3 = f32[204,720]{1,0:T(8,128)S(1)} copy-done((f32[204,720]{1,0:T(8,128)S(1)}, f32[204,720]{1,0:T(8,128)}, u32[]{:S(2)}) %copy-start.3) | copy-done | bytes 587544
  19.5 0.8 %fusion.43 = f32[128,720]{0,1:T(8,128)S(1)} fusion(f32[128,204]{0,1:T(8,128)S(1)} %collective-permute-done.2, f32[204,720]{1,0:T(8,128)S(1)} %copy-done.3), kind=kOutput, calls=%fused_computation.87 | convolution fusion | flops 112803840 | bytes 1060608 | tf_op jit(solution)/shard_map/dot_general | solution.py:184
  20.3 0.0 copy-start.1
  20.3 0.0 copy-start.6
  20.3 0.0 copy-start.7
  20.4 0.8 %fusion.42 = f32[128,720]{0,1:T(8,128)S(1)} fusion(f32[128,204]{0,1:T(8,128)S(1)} %collective-permute-done.1, f32[204,720]{1,0:T(8,128)S(1)} %copy-done.2), kind=kOutput, calls=%fused_computation.86 | convolution fusion | flops 112803840 | bytes 1060608 | tf_op jit(solution)/shard_map/dot_general | solution.py:184
  21.1 0.0 copy-start.4
  21.2 0.2 copy-done.1
  21.4 0.9 %fusion.3 = f32[128,720]{0,1:T(8,128)S(1)} fusion(f32[128,720]{0,1:T(8,128)S(1)} %fusion.43, f32[128,720]{0,1:T(8,128)S(1)} %fusion.42, f32[128,720]{0,1:T(8,128)S(1)} %convolution_add_fusion, f32[128,204]{0,1:T(8,128)S(1)} %collective-permute-done, f32[204,720]{1,0:T(8,128)S(1)} %copy-done.1, f32[720]{0:T(1024)S(1)} %copy-done.6, s32[128]{0:T(128)S(1)} %tile.10, ...), kind=kOutput, calls=%fused_computation.6 | convolution fusion | flops 113356800 | bytes 2172800 | tf_op jit(solution)/shard_map/dot_general | solution.py:184
  22.3 0.4 %maximum_select_fusion = f32[128,181]{0,1:T(8,128)S(1)} fusion(f32[128,180]{0,1:T(8,128)S(1)} %copy.33, f32[128,1]{0,1:T(1,128)S(1)} %slice.201, pred[128]{0:T(512)(128)(4,1)S(1)} %broadcast_compare_fusion.1, f32[128,720]{0,1:T(8,128)S(1)} %fusion.3, f32[181,720]{1,0:T(8,128)S(1)} %copy-done.4), kind=kOutput, calls=%fused_computation.66 | convolution fusion | flops 100132096 | bytes 1075392 | tf_op jit(solution)/shard_map/rw,nw->rn/dot_general | solution.py:187
  22.7 0.1 copy.35
  22.9 0.1 reshape.77
  23.0 0.2 copy.37
  23.2 0.1 reshape.76
  23.2 0.2 copy.36
  23.4 0.1 slice.203
  23.6 0.3 %pad_maximum_fusion.5 = f32[4,4,32,186]{3,2,1,0:T(8,128)S(1)} fusion(f32[4,4,32,3]{3,2,1,0:T(8,128)S(1)} %bitcast.54, f32[4,4,32,180]{3,2,1,0:T(8,128)S(1)} %copy-done, f32[4,4,32,3]{3,2,1,0:T(8,128)S(1)} %slice.203), kind=kLoop, calls=%fused_computation.51 | loop fusion | flops 190464 | bytes 761856 | tf_op jit(solution)/shard_map/concatenate | solution.py:199
  23.8 0.6 %fusion.31 = f32[4,4,32,183]{3,2,1,0:T(8,128)S(1)} fusion(f32[4,4,32,186]{3,2,1,0:T(8,128)S(1)} %pad_maximum_fusion.5, f32[4,4,32,180]{3,2,1,0:T(8,128)S(1)} %copy-done, f32[4,4,32,3]{3,2,1,0:T(8,128)S(1)} %slice.203, f32[4,4,32,3]{3,2,1,0:T(8,128)S(1)} %bitcast.55), kind=kLoop, calls=%fused_computation.50 | loop fusion | flops 655872 | bytes 1505280 | tf_op jit(solution)/shard_map/sub | solution.py:33
  24.4 0.3 %slice_subtract_fusion.3 = (f32[4,4,32,182]{3,2,1,0:T(8,128)S(1)}, f32[4,4,32,182]{3,2,1,0:T(8,128)S(1)}) fusion(f32[4,4,32,183]{3,2,1,0:T(8,128)S(1)} %fusion.31, f32[4,4,32,186]{3,2,1,0:T(8,128)S(1)} %pad_maximum_fusion.5), kind=kLoop, calls=%fused_computation.54 | loop fusion | flops 465920 | bytes 1863680 | tf_op jit(solution)/shard_map/sub | solution.py:43
  24.8 0.8 %slice_bitcast_fusion = f32[4,32,180]{2,1,0:T(8,128)} fusion(f32[4,1,32,181]{3,2,0,1:T(8,128)S(1)} %bitcast.52), kind=kLoop, calls=%fused_computation.60 | loop fusion | bytes 184320 | tf_op jit(solution)/shard_map/squeeze | solution.py:202
  25.5 0.5 %fusion.25 = f32[4,4,32,181]{3,2,1,0:T(8,128)S(1)} fusion(f32[4,4,32,182]{3,2,1,0:T(8,128)S(1)} %get-tuple-element.7, f32[4,4,32,182]{3,2,1,0:T(8,128)S(1)} %get-tuple-element.6, f32[4,4,32,183]{3,2,1,0:T(8,128)S(1)} %fusion.31, f32[4,32,181]{2,1,0:T(8,128)S(1)} %get-tuple-element.19, f32[4,32,181]{2,1,0:T(8,128)S(1)} %get-tuple-element.20, ...), kind=kLoop, calls=%fused_computation.41 | loop fusion | flops 926720 | bytes 2617984 | tf_op jit(solution)/shard_map/mul | solution.py:53
  26.0 1.0 %fusion.20 = f32[4,4,32,180]{3,2,1,0:T(8,128)} fusion(f32[4,4,32,180]{3,2,1,0:T(8,128)S(1)} %copy-done, f32[4,4,33,180]{3,2,1,0:T(8,128)S(1)} %fusion.9, f32[4,4,32,181]{3,2,1,0:T(8,128)S(1)} %fusion.25, f32[32]{0:T(128)S(1)} %fusion.37), kind=kLoop, calls=%fused_computation.34 | loop fusion | flops 460800 | bytes 2211968 | tf_op jit(solution)/shard_map/sub | solution.py:214
  (28 shorter events, 0.4 us)
Async XLA Ops:
  0.6 1.2 %copy-start = (f32[4,4,32,180]{3,2,1,0:T(8,128)S(1)}, f32[4,4,32,180]{3,2,1,0:T(8,128)}, u32[]{:S(2)}) copy-start(f32[4,4,32,180]{3,2,1,0:T(8,128)} %param.7) | copy-start | bytes 1105924
  2.4 12.0 %copy-start.5 = (f32[180,720]{1,0:T(8,128)S(1)}, f32[180,720]{1,0:T(8,128)}, u32[]{:S(2)}) copy-start(f32[180,720]{1,0:T(8,128)} %constant.70) | copy-start | bytes 1555204
  2.6 18.6 %collective-permute-start = (f32[128,204]{0,1:T(8,128)S(1)}, f32[128,204]{0,1:T(8,128)S(1)}, u32[]{:S(2)}, u32[]{:S(2)}) collective-permute-start(f32[128,204]{0,1:T(8,128)S(1)} %pad_maximum_fusion.7), channel_id=1, source_target_pairs={{0,3},{1,0},{2,1},{3,2},{4,7},{5,4},{6,5},{7,6},{8,11},{9,8},{10,9... | collective-permute-start | bytes 313352 | tf_op jit(solution)/shard_map/ppermute | solution.py:162
  3.1 15.8 %collective-permute-start.2 = (f32[128,204]{0,1:T(8,128)S(1)}, f32[128,204]{0,1:T(8,128)S(1)}, u32[]{:S(2)}, u32[]{:S(2)}) collective-permute-start(f32[128,204]{0,1:T(8,128)S(1)} %pad_maximum_fusion.7), channel_id=1, source_target_pairs={{0,1},{1,2},{2,3},{3,0},{4,5},{5,6},{6,7},{7,4},{8,9},{9,10},{10,1... | collective-permute-start | bytes 313352 | tf_op jit(solution)/shard_map/ppermute | solution.py:162
  4.6 15.7 %collective-permute-start.1 = (f32[128,204]{0,1:T(8,128)S(1)}, f32[128,204]{0,1:T(8,128)S(1)}, u32[]{:S(2)}, u32[]{:S(2)}) collective-permute-start(f32[128,204]{0,1:T(8,128)S(1)} %pad_maximum_fusion.7), channel_id=1, source_target_pairs={{0,2},{1,3},{2,0},{3,1},{4,6},{5,7},{6,4},{7,5},{8,10},{9,11},{10,... | collective-permute-start | bytes 313352 | tf_op jit(solution)/shard_map/ppermute | solution.py:162
  9.1 6.4 %collective-permute-start.4 = (f32[4,5,3,180]{3,2,1,0:T(4,128)S(1)}, f32[4,5,3,180]{3,2,1,0:T(4,128)S(1)}, u32[]{:S(2)}, u32[]{:S(2)}) collective-permute-start(f32[4,5,3,180]{3,2,1,0:T(4,128)S(1)} %pad_maximum_fusion.9), channel_id=1, source_target_pairs={{4,0},{8,4},{12,8},{16,12},{20,16},{24,20},{28,24},{5,1},{9,5},{13... | collective-permute-start | bytes 129608 | tf_op jit(solution)/shard_map/ppermute | solution.py:146
  11.1 6.7 %collective-permute-start.3 = (f32[4,5,3,180]{3,2,1,0:T(4,128)S(1)}, f32[4,5,3,180]{3,2,1,0:T(4,128)S(1)}, u32[]{:S(2)}, u32[]{:S(2)}) collective-permute-start(f32[4,5,3,180]{3,2,1,0:T(4,128)S(1)} %pad_maximum_fusion.8), channel_id=1, source_target_pairs={{0,4},{4,8},{8,12},{12,16},{16,20},{20,24},{24,28},{1,5},{5,9},{9,... | collective-permute-start | bytes 129608 | tf_op jit(solution)/shard_map/ppermute | solution.py:145
  13.5 0.7 %copy-start.8 = (s32[256]{0:T(256)S(1)}, s32[256]{0:T(256)}, u32[]{:S(2)}) copy-start(s32[256]{0:T(256)} %param.9) | copy-start | bytes 3076
  18.4 1.1 %copy-start.3 = (f32[204,720]{1,0:T(8,128)S(1)}, f32[204,720]{1,0:T(8,128)}, u32[]{:S(2)}) copy-start(f32[204,720]{1,0:T(8,128)} %constant.69) | copy-start | bytes 1762564
  18.9 1.4 %copy-start.2 = (f32[204,720]{1,0:T(8,128)S(1)}, f32[204,720]{1,0:T(8,128)}, u32[]{:S(2)}) copy-start(f32[204,720]{1,0:T(8,128)} %constant.21) | copy-start | bytes 1762564
  20.3 1.1 %copy-start.1 = (f32[204,720]{1,0:T(8,128)S(1)}, f32[204,720]{1,0:T(8,128)}, u32[]{:S(2)}) copy-start(f32[204,720]{1,0:T(8,128)} %constant.19) | copy-start | bytes 1762564
  20.3 1.1 %copy-start.6 = (f32[720]{0:T(1024)S(1)}, f32[720]{0:T(1024)}, u32[]{:S(2)}) copy-start(f32[720]{0:T(1024)} %constant.15.clone) | copy-start | bytes 8644
  20.3 1.0 %copy-start.7 = (s32[720]{0:T(1024)S(1)}, s32[720]{0:T(1024)}, u32[]{:S(2)}) copy-start(s32[720]{0:T(1024)} %constant.14.clone) | copy-start | bytes 8644
  21.1 1.1 %copy-start.4 = (f32[181,720]{1,0:T(8,128)S(1)}, f32[181,720]{1,0:T(8,128)}, u32[]{:S(2)}) copy-start(f32[181,720]{1,0:T(8,128)} %constant.13.clone) | copy-start | bytes 1563844

commit v7 on v6

--- a/solution.py
+++ b/solution.py
@@ -138,15 +138,14 @@
     zonal = courant[0]
     meridional = courant[1]
     lat_count = lax.axis_size("lat")
-    lat_head = jnp.concatenate([tracers[:, :, :3], meridional[:, None, :3]], axis=1)
+    lat_head = tracers[:, :, :3]
     lat_tail = jnp.concatenate(
         [tracers[:, :, lat_rows - 3 :], meridional[:, None, lat_rows - 3 :]], axis=1
     )
     from_north = lax.ppermute(lat_tail, "lat", [(i, i + 1) for i in range(lat_count - 1)])
     from_south = lax.ppermute(lat_head, "lat", [(i + 1, i) for i in range(lat_count - 1)])
-    lat_ext = jnp.concatenate(
-        [from_north, jnp.concatenate([tracers, meridional[:, None]], axis=1), from_south], axis=2
-    )
+    lat_ext = jnp.concatenate([from_north[:, :tracer_count], tracers, from_south], axis=2)
+    north_faces = jnp.concatenate([from_north[:, tracer_count:, 2:], meridional[:, None]], axis=2)
     flat_count = levels * lat_rows
     flat_zonal = zonal.reshape(flat_count, lon_cols)
     edges = jnp.concatenate([tracers[..., :3], tracers[..., lon_cols - 3 :]], axis=-1)
@@ -203,7 +202,7 @@
     flux_east = ppm_flux(lon_ext, zonal_faces, 3)
     face_weight, cell_weight = metric_weights(band_index * lat_rows, lat_rows, grid_rows)
     flux_north = (
-        ppm_flux(lat_ext[:, :tracer_count], lat_ext[:, tracer_count:, 2 : lat_rows + 3, :], 2)
+        ppm_flux(lat_ext, north_faces, 2)
         * face_weight[None, None, :, None]
     )
     change = (

time: 27.3 us -> 27.3 us (level)
  no operation moved by 1% of the time
where the time goes in v7:
time: 27.3 us; the launch traced here: 27.1 us
  starting transfers between devices  10.8 us (40%)
  local copies, waits for them, and re-layouts  5.1 us (19%)
  other arithmetic  4.01 us (15%)
  matrix products  3.92 us (14%)
  waiting for transfers between devices  2.22 us (8%)
  between operations  1.02 us (4%)
    ppermute x3, starting transfers between devices, body(): lax.ppermute(payload, 'lon', [(i, (i - s) % lon_groups) for i in range(lo...  6.47 us
    dot_general x3, matrix products, body(): coeff = coeff + jnp.dot(received[s], forward[s], precision=high)  2.43 us
    ppermute x1, starting transfers between devices, body(): lax.ppermute(lat_tail, 'lat', [(i, i + 1) for i in range(lat_count - 1)])  2.39 us
    ppermute x1, waiting for transfers between devices, body(): lax.ppermute(lat_tail, 'lat', [(i, i + 1) for i in range(lat_count - 1)])  2.21 us
    unnamed x20, local copies, waits for them, and re-layouts  1.97 us
    ppermute x1, starting transfers between devices, body(): lax.ppermute(lat_head, 'lat', [(i + 1, i) for i in range(lat_count - 1)])  1.94 us
    dot_general x2, matrix products, body(): coeff = jnp.dot(received[0], forward[0], precision=high)  1.09 us
    slice x1, local copies, waits for them, and re-layouts, body(): zonal = courant[0]  1.05 us
  transfers between devices with their start and end apart: 5, of which 1 were waited for; matrix products, arithmetic and copies ran while one was open for 15% of the time, Pallas kernels for 0%

profile of v7, /device:TPU:12, one launch (start us, length us, event | category | flops | bytes accessed | tf_op | source)
XLA Modules:
  0.0 27.1 jit_solution(17818185910319711059)
XLA Ops:
  0.6 1.1 %fusion.42 = (f32[1,4,32,180]{3,2,1,0:T(8,128)S(1)}, f32[4,1,32,180]{3,2,0,1:T(8,128)S(1)}, f32[4,32,180]{2,1,0:T(8,128)S(1)}) fusion(f32[2,4,32,180]{3,2,1,0:T(8,128)} %param.8), kind=kLoop, calls=%fused_computation.82 | loop fusion | bytes 460800 | tf_op jit(solution)/shard_map/slice | solution.py:138
  1.7 0.1 copy-done
  1.8 0.1 fusion.40
  1.9 0.2 copy.39
  2.1 0.2 copy.38
  2.3 0.0 copy-start.5
  2.4 0.1 reshape.151
  2.4 0.1 copy.31
  2.6 0.5 %collective-permute-start = (f32[128,204]{0,1:T(8,128)S(1)}, f32[128,204]{0,1:T(8,128)S(1)}, u32[]{:S(2)}, u32[]{:S(2)}) collective-permute-start(f32[128,204]{0,1:T(8,128)S(1)} %pad_maximum_fusion.3), channel_id=1, source_target_pairs={{0,3},{1,0},{2,1},{3,2},{4,7},{5,4},{6,5},{7,6},{8,11},{9,8},{10,9... | collective-permute-start | bytes 313352 | tf_op jit(solution)/shard_map/ppermute | solution.py:161
  3.1 1.6 %collective-permute-start.2 = (f32[128,204]{0,1:T(8,128)S(1)}, f32[128,204]{0,1:T(8,128)S(1)}, u32[]{:S(2)}, u32[]{:S(2)}) collective-permute-start(f32[128,204]{0,1:T(8,128)S(1)} %pad_maximum_fusion.3), channel_id=1, source_target_pairs={{0,1},{1,2},{2,3},{3,0},{4,5},{5,6},{6,7},{7,4},{8,9},{9,10},{10,1... | collective-permute-start | bytes 313352 | tf_op jit(solution)/shard_map/ppermute | solution.py:161
  4.6 4.4 %collective-permute-start.1 = (f32[128,204]{0,1:T(8,128)S(1)}, f32[128,204]{0,1:T(8,128)S(1)}, u32[]{:S(2)}, u32[]{:S(2)}) collective-permute-start(f32[128,204]{0,1:T(8,128)S(1)} %pad_maximum_fusion.3), channel_id=1, source_target_pairs={{0,2},{1,3},{2,0},{3,1},{4,6},{5,7},{6,4},{7,5},{8,10},{9,11},{10,... | collective-permute-start | bytes 313352 | tf_op jit(solution)/shard_map/ppermute | solution.py:161
  9.1 1.9 %collective-permute-start.4 = (f32[4,4,3,180]{3,2,1,0:T(4,128)S(1)}, f32[4,4,3,180]{3,2,1,0:T(4,128)S(1)}, u32[]{:S(2)}, u32[]{:S(2)}) collective-permute-start(f32[4,4,3,180]{3,2,1,0:T(4,128)S(1)} %get-tuple-element.9), channel_id=1, source_target_pairs={{4,0},{8,4},{12,8},{16,12},{20,16},{24,20},{28,24},{5,1},{9,5},{13... | collective-permute-start | bytes 103688 | tf_op jit(solution)/shard_map/ppermute | solution.py:146
  11.1 2.4 %collective-permute-start.3 = (f32[4,5,3,180]{3,2,1,0:T(4,128)S(1)}, f32[4,5,3,180]{3,2,1,0:T(4,128)S(1)}, u32[]{:S(2)}, u32[]{:S(2)}) collective-permute-start(f32[4,5,3,180]{3,2,1,0:T(4,128)S(1)} %pad_maximum_fusion.4), channel_id=1, source_target_pairs={{0,4},{4,8},{8,12},{12,16},{16,20},{20,24},{24,28},{1,5},{5,9},{9,... | collective-permute-start | bytes 129608 | tf_op jit(solution)/shard_map/ppermute | solution.py:145
  13.5 0.0 copy-start.8
  13.5 0.7 %copy-done.8 = s32[256]{0:T(256)S(1)} copy-done((s32[256]{0:T(256)S(1)}, s32[256]{0:T(256)}, u32[]{:S(2)}) %copy-start.8) | copy-done | bytes 1048
  14.2 0.1 dynamic_slice.3
  14.3 0.1 tile.10
  14.4 0.8 %convolution_bitcast_fusion = f32[128,720]{0,1:T(8,128)S(1)} fusion(f32[180,720]{1,0:T(8,128)S(1)} %copy-done.5, f32[128,180]{1,0:T(8,128)S(1)} %bitcast.48), kind=kOutput, calls=%fused_computation.1 | convolution fusion | flops 99532800 | bytes 979200 | tf_op jit(solution)/shard_map/dot_general | solution.py:181
  15.2 0.3 %convolution_add_fusion = f32[128,720]{0,1:T(8,128)S(1)} fusion(f32[128,720]{0,1:T(8,128)S(1)} %convolution_bitcast_fusion, f32[128,24]{0,1:T(8,128)S(1)} %reshape.151), kind=kOutput, calls=%fused_computation | convolution fusion | flops 13363200 | bytes 749568 | tf_op jit(solution)/shard_map/dot_general | solution.py:181
  15.5 2.2 %collective-permute-done.3 = f32[4,5,3,180]{3,2,1,0:T(4,128)S(1)} collective-permute-done((f32[4,5,3,180]{3,2,1,0:T(4,128)S(1)}, f32[4,5,3,180]{3,2,1,0:T(4,128)S(1)}, u32[]{:S(2)}, u32[]{:S(2)}) %collective-permute-start.3) | collective-permute-done | bytes 43232 | tf_op jit(solution)/shard_map/ppermute | solution.py:145
  17.9 0.1 pad_maximum_fusion
  18.0 0.3 fusion.15
  18.2 0.2 slice_subtract_fusion
  18.5 0.0 copy-start.3
  18.5 0.4 %fusion.9 = f32[4,4,33,180]{3,2,1,0:T(8,128)S(1)} fusion(f32[4,4,34,180]{3,2,1,0:T(8,128)S(1)} %get-tuple-element.3, f32[4,4,34,180]{3,2,1,0:T(8,128)S(1)} %get-tuple-element.2, f32[4,4,35,180]{3,2,1,0:T(8,128)S(1)} %fusion.15, f32[33]{0:T(128)S(1)} %multiply_sine_fusion, f32[4,33,180]{2,1,0:T(8,128)S(1)} %get-tuple-element.15, ...), kind=kLoop, calls=%fused_computation.13 | loop fusion | flops 1045440 | bytes 2685012 | tf_op jit(solution)/shard_map/mul | solution.py:205
  18.9 0.0 copy-start.2
  18.9 0.6 %copy-done.3 = f32[204,720]{1,0:T(8,128)S(1)} copy-done((f32[204,720]{1,0:T(8,128)S(1)}, f32[204,720]{1,0:T(8,128)}, u32[]{:S(2)}) %copy-start.3) | copy-done | bytes 587544
  19.5 0.8 %fusion.44 = f32[128,720]{0,1:T(8,128)S(1)} fusion(f32[128,204]{0,1:T(8,128)S(1)} %collective-permute-done.2, f32[204,720]{1,0:T(8,128)S(1)} %copy-done.3), kind=kOutput, calls=%fused_computation.84 | convolution fusion | flops 112803840 | bytes 1060608 | tf_op jit(solution)/shard_map/dot_general | solution.py:183
  20.3 0.0 copy-start.1
  20.4 0.0 copy-start.6
  20.4 0.0 copy-start.7
  20.4 0.8 %fusion.43 = f32[128,720]{0,1:T(8,128)S(1)} fusion(f32[128,204]{0,1:T(8,128)S(1)} %collective-permute-done.1, f32[204,720]{1,0:T(8,128)S(1)} %copy-done.2), kind=kOutput, calls=%fused_computation.83 | convolution fusion | flops 112803840 | bytes 1060608 | tf_op jit(solution)/shard_map/dot_general | solution.py:183
  21.2 0.0 copy-start.4
  21.2 0.2 copy-done.1
  21.4 0.9 %fusion.3 = f32[128,720]{0,1:T(8,128)S(1)} fusion(f32[128,720]{0,1:T(8,128)S(1)} %fusion.44, f32[128,720]{0,1:T(8,128)S(1)} %fusion.43, f32[128,720]{0,1:T(8,128)S(1)} %convolution_add_fusion, f32[128,204]{0,1:T(8,128)S(1)} %collective-permute-done, f32[204,720]{1,0:T(8,128)S(1)} %copy-done.1, f32[720]{0:T(1024)S(1)} %copy-done.6, s32[128]{0:T(128)S(1)} %tile.10, ...), kind=kOutput, calls=%fused_computation.6 | convolution fusion | flops 113356800 | bytes 2172800 | tf_op jit(solution)/shard_map/dot_general | solution.py:183
  22.3 0.4 %maximum_select_fusion = f32[128,181]{0,1:T(8,128)S(1)} fusion(f32[128,180]{0,1:T(8,128)S(1)} %copy.31, f32[128,1]{0,1:T(1,128)S(1)} %slice.188, pred[128]{0:T(512)(128)(4,1)S(1)} %broadcast_compare_fusion.1, f32[128,720]{0,1:T(8,128)S(1)} %fusion.3, f32[181,720]{1,0:T(8,128)S(1)} %copy-done.4), kind=kOutput, calls=%fused_computation.63 | convolution fusion | flops 100132096 | bytes 1075392 | tf_op jit(solution)/shard_map/rw,nw->rn/dot_general | solution.py:186
  22.7 0.1 copy.33
  22.9 0.1 reshape.153
  23.0 0.2 copy.35
  23.2 0.1 reshape.152
  23.3 0.2 copy.34
  23.5 0.1 slice.190
  23.6 0.3 %pad_maximum_fusion.1 = f32[4,4,32,186]{3,2,1,0:T(8,128)S(1)} fusion(f32[4,4,32,3]{3,2,1,0:T(8,128)S(1)} %bitcast.45, f32[4,4,32,180]{3,2,1,0:T(8,128)S(1)} %copy-done, f32[4,4,32,3]{3,2,1,0:T(8,128)S(1)} %slice.190), kind=kLoop, calls=%fused_computation.47 | loop fusion | flops 190464 | bytes 761856 | tf_op jit(solution)/shard_map/concatenate | solution.py:198
  23.9 0.6 %fusion.30 = f32[4,4,32,183]{3,2,1,0:T(8,128)S(1)} fusion(f32[4,4,32,186]{3,2,1,0:T(8,128)S(1)} %pad_maximum_fusion.1, f32[4,4,32,180]{3,2,1,0:T(8,128)S(1)} %copy-done, f32[4,4,32,3]{3,2,1,0:T(8,128)S(1)} %slice.190, f32[4,4,32,3]{3,2,1,0:T(8,128)S(1)} %bitcast.46), kind=kLoop, calls=%fused_computation.46 | loop fusion | flops 655872 | bytes 1505280 | tf_op jit(solution)/shard_map/sub | solution.py:33
  24.4 0.3 %slice_subtract_fusion.3 = (f32[4,4,32,182]{3,2,1,0:T(8,128)S(1)}, f32[4,4,32,182]{3,2,1,0:T(8,128)S(1)}) fusion(f32[4,4,32,183]{3,2,1,0:T(8,128)S(1)} %fusion.30, f32[4,4,32,186]{3,2,1,0:T(8,128)S(1)} %pad_maximum_fusion.1), kind=kLoop, calls=%fused_computation.50 | loop fusion | flops 465920 | bytes 1863680 | tf_op jit(solution)/shard_map/sub | solution.py:43
  24.8 0.8 %slice_bitcast_fusion = f32[4,32,180]{2,1,0:T(8,128)} fusion(f32[4,1,32,181]{3,2,0,1:T(8,128)S(1)} %bitcast.43), kind=kLoop, calls=%fused_computation.55 | loop fusion | bytes 184320 | tf_op jit(solution)/shard_map/squeeze | solution.py:201
  25.5 0.5 %fusion.24 = f32[4,4,32,181]{3,2,1,0:T(8,128)S(1)} fusion(f32[4,4,32,182]{3,2,1,0:T(8,128)S(1)} %get-tuple-element.5, f32[4,4,32,182]{3,2,1,0:T(8,128)S(1)} %get-tuple-element.4, f32[4,4,32,183]{3,2,1,0:T(8,128)S(1)} %fusion.30, f32[4,32,181]{2,1,0:T(8,128)S(1)} %get-tuple-element.17, f32[4,32,181]{2,1,0:T(8,128)S(1)} %get-tuple-element.18, ...), kind=kLoop, calls=%fused_computation.37 | loop fusion | flops 926720 | bytes 2617984 | tf_op jit(solution)/shard_map/mul | solution.py:53
  26.0 1.0 %fusion.19 = f32[4,4,32,180]{3,2,1,0:T(8,128)} fusion(f32[4,4,32,180]{3,2,1,0:T(8,128)S(1)} %copy-done, f32[4,4,33,180]{3,2,1,0:T(8,128)S(1)} %fusion.9, f32[4,4,32,181]{3,2,1,0:T(8,128)S(1)} %fusion.24, f32[32]{0:T(128)S(1)} %fusion.38), kind=kLoop, calls=%fused_computation.30 | loop fusion | flops 460800 | bytes 2211968 | tf_op jit(solution)/shard_map/sub | solution.py:213
  (30 shorter events, 0.5 us)
Async XLA Ops:
  0.6 1.2 %copy-start = (f32[4,4,32,180]{3,2,1,0:T(8,128)S(1)}, f32[4,4,32,180]{3,2,1,0:T(8,128)}, u32[]{:S(2)}) copy-start(f32[4,4,32,180]{3,2,1,0:T(8,128)} %param.7) | copy-start | bytes 1105924
  2.3 12.1 %copy-start.5 = (f32[180,720]{1,0:T(8,128)S(1)}, f32[180,720]{1,0:T(8,128)}, u32[]{:S(2)}) copy-start(f32[180,720]{1,0:T(8,128)} %constant.70) | copy-start | bytes 1555204
  2.6 18.6 %collective-permute-start = (f32[128,204]{0,1:T(8,128)S(1)}, f32[128,204]{0,1:T(8,128)S(1)}, u32[]{:S(2)}, u32[]{:S(2)}) collective-permute-start(f32[128,204]{0,1:T(8,128)S(1)} %pad_maximum_fusion.3), channel_id=1, source_target_pairs={{0,3},{1,0},{2,1},{3,2},{4,7},{5,4},{6,5},{7,6},{8,11},{9,8},{10,9... | collective-permute-start | bytes 313352 | tf_op jit(solution)/shard_map/ppermute | solution.py:161
  3.1 15.9 %collective-permute-start.2 = (f32[128,204]{0,1:T(8,128)S(1)}, f32[128,204]{0,1:T(8,128)S(1)}, u32[]{:S(2)}, u32[]{:S(2)}) collective-permute-start(f32[128,204]{0,1:T(8,128)S(1)} %pad_maximum_fusion.3), channel_id=1, source_target_pairs={{0,1},{1,2},{2,3},{3,0},{4,5},{5,6},{6,7},{7,4},{8,9},{9,10},{10,1... | collective-permute-start | bytes 313352 | tf_op jit(solution)/shard_map/ppermute | solution.py:161
  4.6 15.7 %collective-permute-start.1 = (f32[128,204]{0,1:T(8,128)S(1)}, f32[128,204]{0,1:T(8,128)S(1)}, u32[]{:S(2)}, u32[]{:S(2)}) collective-permute-start(f32[128,204]{0,1:T(8,128)S(1)} %pad_maximum_fusion.3), channel_id=1, source_target_pairs={{0,2},{1,3},{2,0},{3,1},{4,6},{5,7},{6,4},{7,5},{8,10},{9,11},{10,... | collective-permute-start | bytes 313352 | tf_op jit(solution)/shard_map/ppermute | solution.py:161
  9.1 8.8 %collective-permute-start.4 = (f32[4,4,3,180]{3,2,1,0:T(4,128)S(1)}, f32[4,4,3,180]{3,2,1,0:T(4,128)S(1)}, u32[]{:S(2)}, u32[]{:S(2)}) collective-permute-start(f32[4,4,3,180]{3,2,1,0:T(4,128)S(1)} %get-tuple-element.9), channel_id=1, source_target_pairs={{4,0},{8,4},{12,8},{16,12},{20,16},{24,20},{28,24},{5,1},{9,5},{13... | collective-permute-start | bytes 103688 | tf_op jit(solution)/shard_map/ppermute | solution.py:146
  11.1 6.7 %collective-permute-start.3 = (f32[4,5,3,180]{3,2,1,0:T(4,128)S(1)}, f32[4,5,3,180]{3,2,1,0:T(4,128)S(1)}, u32[]{:S(2)}, u32[]{:S(2)}) collective-permute-start(f32[4,5,3,180]{3,2,1,0:T(4,128)S(1)} %pad_maximum_fusion.4), channel_id=1, source_target_pairs={{0,4},{4,8},{8,12},{12,16},{16,20},{20,24},{24,28},{1,5},{5,9},{9,... | collective-permute-start | bytes 129608 | tf_op jit(solution)/shard_map/ppermute | solution.py:145
  13.5 0.7 %copy-start.8 = (s32[256]{0:T(256)S(1)}, s32[256]{0:T(256)}, u32[]{:S(2)}) copy-start(s32[256]{0:T(256)} %param.9) | copy-start | bytes 3076
  18.5 1.1 %copy-start.3 = (f32[204,720]{1,0:T(8,128)S(1)}, f32[204,720]{1,0:T(8,128)}, u32[]{:S(2)}) copy-start(f32[204,720]{1,0:T(8,128)} %constant.69) | copy-start | bytes 1762564
  18.9 1.4 %copy-start.2 = (f32[204,720]{1,0:T(8,128)S(1)}, f32[204,720]{1,0:T(8,128)}, u32[]{:S(2)}) copy-start(f32[204,720]{1,0:T(8,128)} %constant.21) | copy-start | bytes 1762564
  20.3 1.1 %copy-start.1 = (f32[204,720]{1,0:T(8,128)S(1)}, f32[204,720]{1,0:T(8,128)}, u32[]{:S(2)}) copy-start(f32[204,720]{1,0:T(8,128)} %constant.19) | copy-start | bytes 1762564
  20.4 1.1 %copy-start.6 = (f32[720]{0:T(1024)S(1)}, f32[720]{0:T(1024)}, u32[]{:S(2)}) copy-start(f32[720]{0:T(1024)} %constant.15.clone) | copy-start | bytes 8644
  20.4 1.0 %copy-start.7 = (s32[720]{0:T(1024)S(1)}, s32[720]{0:T(1024)}, u32[]{:S(2)}) copy-start(s32[720]{0:T(1024)} %constant.14.clone) | copy-start | bytes 8644
  21.2 1.1 %copy-start.4 = (f32[181,720]{1,0:T(8,128)S(1)}, f32[181,720]{1,0:T(8,128)}, u32[]{:S(2)}) copy-start(f32[181,720]{1,0:T(8,128)} %constant.13.clone) | copy-start | bytes 1563844
